TPU v7x, 512 devices: a whole 4x4x16 slice. The times are simulated.
512 devices in a mesh: sec: 32 (over z_lo, x), tile: 16 (over y, z_hi, core).
Axes of the slice: x: 4, y: 4, z: 16 (z_hi: 2, z_lo: 8; z = z_hi * 8 + z_lo), core: 2. Of those that a mesh axis runs over, the one named last changes fastest.
Arguments:
- images: bfloat16 [192, 8192, 512], P('sec', 'tile'), may hold values from -24 to 24
- displacement: float32 [192, 2, 2048, 128], P('sec', None, 'tile'), may hold values from -6 to 6
- offsets: int32 [192, 3, 2], P('sec'), may hold values from 0 to 3
- weights: int32 [192, 3], P('sec'), may hold values from 1 to 3
- stiffness: float32 [192], P('sec'), may hold values from 0.25 to 1
Outputs:
- aligned: float32 [192, 2, 2048, 128], P('sec', None, 'tile')
All inputs are finite; a program needn't handle non-finite values.
Results may differ from a plain program's by a relative error of at most 0.005.
Values may be sent and summed in bfloat16 or wider, within the bound.
A program may use at most 64 MiB of HBM per device.

v0:
```python
import jax
import jax.numpy as jnp
from jax import lax
from jax.sharding import PartitionSpec as P

PIXELS = 512
GRID = 128
SKIPS = 3
ITERS = 3


kernel_sigma = 2.0
force_step = 0.5
elastic_step = 0.1


def from_behind(value, axis, steps):
    count = lax.axis_size(axis)
    initial, last = (max(0, -steps), min(count, count - steps))
    return lax.ppermute(value, axis, [(source, source + steps) for source in range(initial, last)])


def with_halo(block, sides, width):
    for axis, dim in sides:
        count = lax.axis_size(axis)
        forward = [(i, i + 1) for i in range(count - 1)]
        backward = [(target, source) for source, target in forward]
        low = lax.ppermute(
            lax.slice_in_dim(block, block.shape[dim] - width, None, axis=dim), axis, forward
        )
        high = lax.ppermute(lax.slice_in_dim(block, 0, width, axis=dim), axis, backward)
        block = jnp.concatenate([low, block, high], axis=dim)
    return block


def kernel_tables(offset, cells, pixels):
    spacing = pixels // cells
    centres = jnp.arange(cells, dtype=jnp.float32)[:, None]
    columns = jnp.arange(pixels, dtype=jnp.float32)[None, :]
    offset_value = jnp.asarray(offset).astype(jnp.float32)
    spread = columns - (spacing * centres + (spacing - 1) / 2.0 + offset_value)
    kernel = jnp.exp(-spread * spread / (2.0 * kernel_sigma * kernel_sigma))
    smooth = kernel / jnp.sum(kernel, axis=1, keepdims=True)
    slopes = smooth * spread / (kernel_sigma * kernel_sigma)
    return (smooth.astype(jnp.bfloat16), slopes.astype(jnp.bfloat16))


def pair_cache(picture, offset_rows, offset_cols):
    row_smooth, row_slopes = kernel_tables(offset_rows, GRID, PIXELS)
    col_smooth, col_slopes = kernel_tables(offset_cols, GRID, PIXELS)
    col_tables = jnp.concatenate([col_smooth, col_slopes], axis=0)
    halfway = lax.dot_general(
        picture, col_tables, (((1,), (1,)), ((), ())), preferred_element_type=jnp.float32
    ).astype(jnp.bfloat16)
    row_tables = jnp.concatenate([row_smooth, row_slopes], axis=0)
    pooled_rows = jnp.dot(row_tables, halfway[:, :GRID], preferred_element_type=jnp.float32)
    across = jnp.dot(row_smooth, halfway[:, GRID:], preferred_element_type=jnp.float32)
    return jnp.stack([pooled_rows[:GRID], pooled_rows[GRID:], across]).astype(jnp.bfloat16)


def own_pool(picture):
    smooth, slopes = kernel_tables(0, GRID, PIXELS)
    halfway = lax.dot_general(
        picture, smooth, (((1,), (1,)), ((), ())), preferred_element_type=jnp.float32
    ).astype(jnp.bfloat16)
    return jnp.dot(smooth, halfway, preferred_element_type=jnp.float32).astype(jnp.bfloat16)


def pair_force(cached_pair, pooled, field_later, field_earlier, weighting):
    cached = cached_pair.astype(jnp.float32)
    mismatch = (
        cached[0]
        - pooled
        + cached[1] * (field_later[0] - field_earlier[0])
        + cached[2] * (field_later[1] - field_earlier[1])
    )
    robust = mismatch / (1.0 + mismatch * mismatch)
    return (weighting * robust)[None] * cached[1:3]


def local(images, displacement, offsets, weights, stiffness):
    resident = images.shape[0]
    section_base = lax.axis_index("sec") * resident
    sections = resident * lax.axis_size("sec")
    pooled_half = jnp.stack([own_pool(images[section]) for section in range(resident)])
    own_pooled = pooled_half.astype(jnp.float32)
    arriving = from_behind(images[:SKIPS], "sec", -1)
    widened = jnp.concatenate([images, arriving], axis=0)
    caches = [
        [
            pair_cache(
                widened[section + stride],
                offsets[section, stride - 1, 0],
                offsets[section, stride - 1, 1],
            )
            for stride in range(1, SKIPS + 1)
        ]
        for section in range(resident)
    ]
    current = displacement
    for step_index in range(ITERS):
        rim = with_halo(current.astype(jnp.bfloat16), (("tile", 2),), 1).astype(current.dtype)
        ahead = from_behind(current[:SKIPS], "sec", -1)
        widened_field = jnp.concatenate([current, ahead], axis=0)
        forces = [jnp.zeros_like(current[0]) for section in range(resident)]
        returning = [jnp.zeros_like(current[0]) for section in range(SKIPS)]
        for section in range(resident):
            for stride in range(1, SKIPS + 1):
                present = (section_base + section + stride < sections).astype(jnp.float32)
                weighting = weights[section, stride - 1].astype(jnp.float32) * present
                pulled = pair_force(
                    caches[section][stride - 1],
                    own_pooled[section],
                    widened_field[section + stride],
                    current[section],
                    weighting,
                )
                forces[section] = forces[section] + pulled
                target = section + stride
                if target < resident:
                    forces[target] = forces[target] - pulled
                else:
                    returning[target - resident] = returning[target - resident] - pulled
        stacked_forces = jnp.stack(forces)
        returned = from_behind(jnp.stack(returning), "sec", 1)
        stacked_forces = jnp.concatenate(
            [stacked_forces[:SKIPS] + returned, stacked_forces[SKIPS:]], axis=0
        )
        col_padded = jnp.pad(current, ((0, 0), (0, 0), (0, 0), (1, 1)))
        beside_all = (
            rim[:, :, 2:, :]
            + rim[:, :, :-2, :]
            + col_padded[:, :, :, 2:]
            + col_padded[:, :, :, :-2]
        )
        laplacian = 4.0 * current - beside_all
        current = (
            current
            + force_step * stacked_forces
            - elastic_step * stiffness[:, None, None, None] * laplacian
        )
    return current


def solution(mesh):
    placed = (
        P("sec", "tile", None),
        P("sec", None, "tile", None),
        P("sec", None, None),
        P("sec", None),
        P("sec"),
    )
    return jax.shard_map(
        local, mesh=mesh, in_specs=placed, out_specs=P("sec", None, "tile", None), check_vma=False
    )
```

profile of v0, /device:TPU:153, one launch (start us, length us, event | category | flops | bytes accessed | tf_op | source)
XLA Modules:
  0.0 226.0 jit_solution(1970505078074244176)
XLA Ops:
  1.9 2.6 %collective-permute-start.4 = (bf16[6,2,1,128]{3,2,1,0:T(2,128)(2,1)}, bf16[6,2,1,128]{3,2,1,0:T(2,128)(2,1)S(1)}, u32[]{:S(2)}, u32[]{:S(2)}) collective-permute-start(bf16[6,2,1,128]{3,2,1,0:T(2,128)(2,1)} %get-tuple-element.68), channel_id=1, source_target_pairs={{1,0},{2,1},{3,2},{4,3},{5,4},{6,5},{7,6},{8,7},{9,8},{10,9},{11,1... | collective-permute-start | bytes 9224 | tf_op jit(solution)/shard_map/ppermute | solution.py:31
  4.5 11.7 %collective-permute-start.3 = (bf16[6,2,1,128]{3,2,1,0:T(2,128)(2,1)}, bf16[6,2,1,128]{3,2,1,0:T(2,128)(2,1)S(1)}, u32[]{:S(2)}, u32[]{:S(2)}) collective-permute-start(bf16[6,2,1,128]{3,2,1,0:T(2,128)(2,1)} %get-tuple-element.67), channel_id=1, source_target_pairs={{0,1},{1,2},{2,3},{3,4},{4,5},{5,6},{6,7},{7,8},{8,9},{9,10},{10,1... | collective-permute-start | bytes 9224 | tf_op jit(solution)/shard_map/ppermute | solution.py:28
  16.2 2.7 %slice.1659 = bf16[3,512,512]{2,1,0:T(8,128)(2,1)} slice(bf16[6,512,512]{2,1,0:T(8,128)(2,1)} %param.5), slice={[0:3], [0:512], [0:512]} | slice | bytes 3145728 | tf_op jit(solution)/shard_map/slice | solution.py:87
  18.8 4.9 %collective-permute-start = (bf16[3,512,512]{2,1,0:T(8,128)(2,1)}, bf16[3,512,512]{2,1,0:T(8,128)(2,1)}, u32[]{:S(2)}, u32[]{:S(2)}) collective-permute-start(bf16[3,512,512]{2,1,0:T(8,128)(2,1)} %slice.1659), channel_id=1, source_target_pairs={{16,0},{32,16},{48,32},{64,48},{80,64},{96,80},{112,96},{128,112},... | collective-permute-start | bytes 4718600 | tf_op jit(solution)/shard_map/ppermute | solution.py:20
  24.5 2.4 %collective-permute-start.1 = (f32[3,2,128,128]{3,2,1,0:T(8,128)}, f32[3,2,128,128]{3,2,1,0:T(8,128)}, u32[]{:S(2)}, u32[]{:S(2)}) collective-permute-start(f32[3,2,128,128]{3,2,1,0:T(8,128)} %slice.1668), channel_id=1, source_target_pairs={{16,0},{32,16},{48,32},{64,48},{80,64},{96,80},{112,96},{128,112},... | collective-permute-start | bytes 1179656 | tf_op jit(solution)/shard_map/ppermute | solution.py:20
  36.3 1.5 fusion.49
  37.8 1.5 fusion.51
  39.4 1.5 fusion.53
  40.9 1.5 fusion.55
  42.5 1.5 fusion.57
  44.0 1.5 fusion.59
  74.9 1.4 fusion.3
  115.8 1.4 fusion.10
  117.9 1.4 fusion.14
  119.9 1.4 fusion.12
  122.0 1.4 fusion.13
  124.1 1.4 fusion.9
  131.5 2.8 %collective-permute-start.2 = (f32[3,2,128,128]{3,2,1,0:T(8,128)S(1)}, f32[3,2,128,128]{3,2,1,0:T(8,128)S(1)}, u32[]{:S(2)}, u32[]{:S(2)}) collective-permute-start(f32[3,2,128,128]{3,2,1,0:T(8,128)S(1)} %pad_maximum_fusion), channel_id=1, source_target_pairs={{0,16},{16,32},{32,48},{48,64},{64,80},{80,96},{96,112},{112,128},... | collective-permute-start | bytes 1179656 | tf_op jit(solution)/shard_map/ppermute | solution.py:20
  134.5 12.3 %collective-permute-done.2 = f32[3,2,128,128]{3,2,1,0:T(8,128)S(1)} collective-permute-done((f32[3,2,128,128]{3,2,1,0:T(8,128)S(1)}, f32[3,2,128,128]{3,2,1,0:T(8,128)S(1)}, u32[]{:S(2)}, u32[]{:S(2)}) %collective-permute-start.2) | collective-permute-done | bytes 393248 | tf_op jit(solution)/shard_map/ppermute | solution.py:20
  147.7 3.3 %collective-permute-start.8 = (bf16[6,2,1,128]{3,2,1,0:T(2,128)(2,1)S(1)}, bf16[6,2,1,128]{3,2,1,0:T(2,128)(2,1)S(1)}, u32[]{:S(2)}, u32[]{:S(2)}) collective-permute-start(bf16[6,2,1,128]{3,2,1,0:T(2,128)(2,1)S(1)} %get-tuple-element.66), channel_id=1, source_target_pairs={{1,0},{2,1},{3,2},{4,3},{5,4},{6,5},{7,6},{8,7},{9,8},{10,9},{11,1... | collective-permute-start | bytes 9224 | tf_op jit(solution)/shard_map/ppermute | solution.py:31
  151.1 10.9 %collective-permute-start.7 = (bf16[6,2,1,128]{3,2,1,0:T(2,128)(2,1)S(1)}, bf16[6,2,1,128]{3,2,1,0:T(2,128)(2,1)S(1)}, u32[]{:S(2)}, u32[]{:S(2)}) collective-permute-start(bf16[6,2,1,128]{3,2,1,0:T(2,128)(2,1)S(1)} %get-tuple-element.65), channel_id=1, source_target_pairs={{0,1},{1,2},{2,3},{3,4},{4,5},{5,6},{6,7},{7,8},{8,9},{9,10},{10,1... | collective-permute-start | bytes 9224 | tf_op jit(solution)/shard_map/ppermute | solution.py:28
  162.0 1.9 collective-permute-start.5
  164.1 8.5 %collective-permute-done.5 = f32[3,2,128,128]{3,2,1,0:T(8,128)S(1)} collective-permute-done((f32[3,2,128,128]{3,2,1,0:T(8,128)S(1)}, f32[3,2,128,128]{3,2,1,0:T(8,128)S(1)}, u32[]{:S(2)}, u32[]{:S(2)}) %collective-permute-start.5) | collective-permute-done | bytes 393248 | tf_op jit(solution)/shard_map/ppermute | solution.py:20
  173.3 1.9 collective-permute-start.6
  175.5 12.9 %collective-permute-done.6 = f32[3,2,128,128]{3,2,1,0:T(8,128)S(1)} collective-permute-done((f32[3,2,128,128]{3,2,1,0:T(8,128)S(1)}, f32[3,2,128,128]{3,2,1,0:T(8,128)S(1)}, u32[]{:S(2)}, u32[]{:S(2)}) %collective-permute-start.6) | collective-permute-done | bytes 393248 | tf_op jit(solution)/shard_map/ppermute | solution.py:20
  189.3 1.9 collective-permute-start.12
  191.2 12.4 %collective-permute-start.11 = (bf16[6,2,1,128]{3,2,1,0:T(2,128)(2,1)S(1)}, bf16[6,2,1,128]{3,2,1,0:T(2,128)(2,1)S(1)}, u32[]{:S(2)}, u32[]{:S(2)}) collective-permute-start(bf16[6,2,1,128]{3,2,1,0:T(2,128)(2,1)S(1)} %get-tuple-element.63), channel_id=1, source_target_pairs={{0,1},{1,2},{2,3},{3,4},{4,5},{5,6},{6,7},{7,8},{8,9},{9,10},{10,1... | collective-permute-start | bytes 9224 | tf_op jit(solution)/shard_map/ppermute | solution.py:28
  203.6 1.9 collective-permute-start.9
  205.7 6.4 %collective-permute-done.9 = f32[3,2,128,128]{3,2,1,0:T(8,128)S(1)} collective-permute-done((f32[3,2,128,128]{3,2,1,0:T(8,128)S(1)}, f32[3,2,128,128]{3,2,1,0:T(8,128)S(1)}, u32[]{:S(2)}, u32[]{:S(2)}) %collective-permute-start.9) | collective-permute-done | bytes 393248 | tf_op jit(solution)/shard_map/ppermute | solution.py:20
  212.7 1.9 collective-permute-start.10
  214.9 9.6 %collective-permute-done.10 = f32[3,2,128,128]{3,2,1,0:T(8,128)S(1)} collective-permute-done((f32[3,2,128,128]{3,2,1,0:T(8,128)S(1)}, f32[3,2,128,128]{3,2,1,0:T(8,128)S(1)}, u32[]{:S(2)}, u32[]{:S(2)}) %collective-permute-start.10) | collective-permute-done | bytes 393248 | tf_op jit(solution)/shard_map/ppermute | solution.py:20
  224.6 1.4 fusion.74
  (370 shorter events, 57.8 us)
Async XLA Ops:
  0.0 23.7 %copy-start = (f32[6,2,128,128]{3,2,1,0:T(8,128)S(1)}, f32[6,2,128,128]{3,2,1,0:T(8,128)}, u32[]{:S(2)}) copy-start(f32[6,2,128,128]{3,2,1,0:T(8,128)} %param.6) | copy-start | bytes 2359300
  0.0 27.0 %copy-start.29 = (s32[6,3,2]{0,2,1:T(2,128)S(1)}, s32[6,3,2]{0,2,1:T(2,128)}, u32[]{:S(2)}) copy-start(s32[6,3,2]{0,2,1:T(2,128)} %param.7) | copy-start | bytes 436
  0.0 35.3 %copy-start.30 = (s32[6,3]{0,1:T(4,128)S(1)}, s32[6,3]{0,1:T(4,128)}, u32[]{:S(2)}) copy-start(s32[6,3]{0,1:T(4,128)} %param.8) | copy-start | bytes 220
  1.9 132.5 %collective-permute-start.4 = (bf16[6,2,1,128]{3,2,1,0:T(2,128)(2,1)}, bf16[6,2,1,128]{3,2,1,0:T(2,128)(2,1)S(1)}, u32[]{:S(2)}, u32[]{:S(2)}) collective-permute-start(bf16[6,2,1,128]{3,2,1,0:T(2,128)(2,1)} %get-tuple-element.68), channel_id=1, source_target_pairs={{1,0},{2,1},{3,2},{4,3},{5,4},{6,5},{7,6},{8,7},{9,8},{10,9},{11,1... | collective-permute-start | bytes 9224 | tf_op jit(solution)/shard_map/ppermute | solution.py:31
  4.5 129.9 %collective-permute-start.3 = (bf16[6,2,1,128]{3,2,1,0:T(2,128)(2,1)}, bf16[6,2,1,128]{3,2,1,0:T(2,128)(2,1)S(1)}, u32[]{:S(2)}, u32[]{:S(2)}) collective-permute-start(bf16[6,2,1,128]{3,2,1,0:T(2,128)(2,1)} %get-tuple-element.67), channel_id=1, source_target_pairs={{0,1},{1,2},{2,3},{3,4},{4,5},{5,6},{6,7},{7,8},{8,9},{9,10},{10,1... | collective-permute-start | bytes 9224 | tf_op jit(solution)/shard_map/ppermute | solution.py:28
  18.8 96.5 %collective-permute-start = (bf16[3,512,512]{2,1,0:T(8,128)(2,1)}, bf16[3,512,512]{2,1,0:T(8,128)(2,1)}, u32[]{:S(2)}, u32[]{:S(2)}) collective-permute-start(bf16[3,512,512]{2,1,0:T(8,128)(2,1)} %slice.1659), channel_id=1, source_target_pairs={{16,0},{32,16},{48,32},{64,48},{80,64},{96,80},{112,96},{128,112},... | collective-permute-start | bytes 4718600 | tf_op jit(solution)/shard_map/ppermute | solution.py:20
  24.5 103.6 %collective-permute-start.1 = (f32[3,2,128,128]{3,2,1,0:T(8,128)}, f32[3,2,128,128]{3,2,1,0:T(8,128)}, u32[]{:S(2)}, u32[]{:S(2)}) collective-permute-start(f32[3,2,128,128]{3,2,1,0:T(8,128)} %slice.1668), channel_id=1, source_target_pairs={{16,0},{32,16},{48,32},{64,48},{80,64},{96,80},{112,96},{128,112},... | collective-permute-start | bytes 1179656 | tf_op jit(solution)/shard_map/ppermute | solution.py:20
  30.7 8.6 %copy-start.31 = (f32[128]{0:T(128)}, f32[128]{0:T(128)S(1)}, u32[]{:S(2)}) copy-start(f32[128]{0:T(128)S(1)} %broadcast_add_fusion.15) | copy-start | bytes 1540
  30.9 8.4 %copy-start.33 = (f32[128]{0:T(128)}, f32[128]{0:T(128)S(1)}, u32[]{:S(2)}) copy-start(f32[128]{0:T(128)S(1)} %fusion.339) | copy-start | bytes 1540
  34.2 5.2 %copy-start.35 = (f32[128]{0:T(128)}, f32[128]{0:T(128)S(1)}, u32[]{:S(2)}) copy-start(f32[128]{0:T(128)S(1)} %broadcast_add_fusion.7) | copy-start | bytes 1540
  34.4 4.9 %copy-start.37 = (f32[128]{0:T(128)}, f32[128]{0:T(128)S(1)}, u32[]{:S(2)}) copy-start(f32[128]{0:T(128)S(1)} %fusion.323) | copy-start | bytes 1540
  45.6 16.3 %copy-start.1 = (bf16[6,512,512]{2,1,0:T(8,128)(2,1)S(1)}, bf16[6,512,512]{2,1,0:T(8,128)(2,1)}, u32[]{:S(2)}) copy-start(bf16[6,512,512]{2,1,0:T(8,128)(2,1)} %param.5) | copy-start | bytes 9437188
  48.1 13.4 %copy-start.39 = (f32[128]{0:T(128)}, f32[128]{0:T(128)S(1)}, u32[]{:S(2)}) copy-start(f32[128]{0:T(128)S(1)} %broadcast_add_fusion.11) | copy-start | bytes 1540
  48.3 13.4 %copy-start.41 = (f32[128]{0:T(128)}, f32[128]{0:T(128)S(1)}, u32[]{:S(2)}) copy-start(f32[128]{0:T(128)S(1)} %fusion.331) | copy-start | bytes 1540
  51.6 10.2 %copy-start.43 = (f32[128]{0:T(128)}, f32[128]{0:T(128)S(1)}, u32[]{:S(2)}) copy-start(f32[128]{0:T(128)S(1)} %broadcast_add_fusion.9) | copy-start | bytes 1540
  51.8 10.0 %copy-start.45 = (f32[128]{0:T(128)}, f32[128]{0:T(128)S(1)}, u32[]{:S(2)}) copy-start(f32[128]{0:T(128)S(1)} %fusion.327) | copy-start | bytes 1540
  55.2 6.7 %copy-start.47 = (f32[128]{0:T(128)}, f32[128]{0:T(128)S(1)}, u32[]{:S(2)}) copy-start(f32[128]{0:T(128)S(1)} %broadcast_add_fusion.17) | copy-start | bytes 1540
  55.4 6.5 %copy-start.49 = (f32[128]{0:T(128)}, f32[128]{0:T(128)S(1)}, u32[]{:S(2)}) copy-start(f32[128]{0:T(128)S(1)} %fusion.343) | copy-start | bytes 1540
  72.0 6.9 %copy-start.2 = (bf16[6,512,512]{2,1,0:T(8,128)(2,1)S(1)}, bf16[6,512,512]{2,1,0:T(8,128)(2,1)}, u32[]{:S(2)}) copy-start(bf16[6,512,512]{2,1,0:T(8,128)(2,1)} %param.5) | copy-start | bytes 9437188
  115.2 4.1 %copy-start.36 = (f32[128]{0:T(128)S(1)}, f32[128]{0:T(128)}, u32[]{:S(2)}) copy-start(f32[128]{0:T(128)} %copy-done.35) | copy-start | bytes 1540
  115.3 4.1 %copy-start.38 = (f32[128]{0:T(128)S(1)}, f32[128]{0:T(128)}, u32[]{:S(2)}) copy-start(f32[128]{0:T(128)} %copy-done.37) | copy-start | bytes 1540
  119.9 3.8 %copy-start.21 = (bf16[128,512]{1,0:T(8,128)(2,1)S(1)}, bf16[128,512]{1,0:T(8,128)(2,1)}, u32[]{:S(2)}) copy-start(bf16[128,512]{1,0:T(8,128)(2,1)} %get-tuple-element.239) | copy-start | bytes 393220
  119.9 3.8 %copy-start.22 = (bf16[128,512]{1,0:T(8,128)(2,1)S(1)}, bf16[128,512]{1,0:T(8,128)(2,1)}, u32[]{:S(2)}) copy-start(bf16[128,512]{1,0:T(8,128)(2,1)} %get-tuple-element.240) | copy-start | bytes 393220
  131.5 15.3 %collective-permute-start.2 = (f32[3,2,128,128]{3,2,1,0:T(8,128)S(1)}, f32[3,2,128,128]{3,2,1,0:T(8,128)S(1)}, u32[]{:S(2)}, u32[]{:S(2)}) collective-permute-start(f32[3,2,128,128]{3,2,1,0:T(8,128)S(1)} %pad_maximum_fusion), channel_id=1, source_target_pairs={{0,16},{16,32},{32,48},{48,64},{64,80},{80,96},{96,112},{112,128},... | collective-permute-start | bytes 1179656 | tf_op jit(solution)/shard_map/ppermute | solution.py:20
  147.7 27.6 %collective-permute-start.8 = (bf16[6,2,1,128]{3,2,1,0:T(2,128)(2,1)S(1)}, bf16[6,2,1,128]{3,2,1,0:T(2,128)(2,1)S(1)}, u32[]{:S(2)}, u32[]{:S(2)}) collective-permute-start(bf16[6,2,1,128]{3,2,1,0:T(2,128)(2,1)S(1)} %get-tuple-element.66), channel_id=1, source_target_pairs={{1,0},{2,1},{3,2},{4,3},{5,4},{6,5},{7,6},{8,7},{9,8},{10,9},{11,1... | collective-permute-start | bytes 9224 | tf_op jit(solution)/shard_map/ppermute | solution.py:31
  151.1 24.3 %collective-permute-start.7 = (bf16[6,2,1,128]{3,2,1,0:T(2,128)(2,1)S(1)}, bf16[6,2,1,128]{3,2,1,0:T(2,128)(2,1)S(1)}, u32[]{:S(2)}, u32[]{:S(2)}) collective-permute-start(bf16[6,2,1,128]{3,2,1,0:T(2,128)(2,1)S(1)} %get-tuple-element.65), channel_id=1, source_target_pairs={{0,1},{1,2},{2,3},{3,4},{4,5},{5,6},{6,7},{7,8},{8,9},{9,10},{10,1... | collective-permute-start | bytes 9224 | tf_op jit(solution)/shard_map/ppermute | solution.py:28
  162.0 10.6 %collective-permute-start.5 = (f32[3,2,128,128]{3,2,1,0:T(8,128)S(1)}, f32[3,2,128,128]{3,2,1,0:T(8,128)S(1)}, u32[]{:S(2)}, u32[]{:S(2)}) collective-permute-start(f32[3,2,128,128]{3,2,1,0:T(8,128)S(1)} %slice.2000), channel_id=1, source_target_pairs={{16,0},{32,16},{48,32},{64,48},{80,64},{96,80},{112,96},{128,112},... | collective-permute-start | bytes 1179656 | tf_op jit(solution)/shard_map/ppermute | solution.py:20
  173.3 15.1 %collective-permute-start.6 = (f32[3,2,128,128]{3,2,1,0:T(8,128)S(1)}, f32[3,2,128,128]{3,2,1,0:T(8,128)S(1)}, u32[]{:S(2)}, u32[]{:S(2)}) collective-permute-start(f32[3,2,128,128]{3,2,1,0:T(8,128)S(1)} %pad_maximum_fusion.1), channel_id=1, source_target_pairs={{0,16},{16,32},{32,48},{48,64},{64,80},{80,96},{96,112},{112,128},... | collective-permute-start | bytes 1179656 | tf_op jit(solution)/shard_map/ppermute | solution.py:20
  189.3 25.5 %collective-permute-start.12 = (bf16[6,2,1,128]{3,2,1,0:T(2,128)(2,1)S(1)}, bf16[6,2,1,128]{3,2,1,0:T(2,128)(2,1)S(1)}, u32[]{:S(2)}, u32[]{:S(2)}) collective-permute-start(bf16[6,2,1,128]{3,2,1,0:T(2,128)(2,1)S(1)} %get-tuple-element.64), channel_id=1, source_target_pairs={{1,0},{2,1},{3,2},{4,3},{5,4},{6,5},{7,6},{8,7},{9,8},{10,9},{11,1... | collective-permute-start | bytes 9224 | tf_op jit(solution)/shard_map/ppermute | solution.py:31
  191.2 23.6 %collective-permute-start.11 = (bf16[6,2,1,128]{3,2,1,0:T(2,128)(2,1)S(1)}, bf16[6,2,1,128]{3,2,1,0:T(2,128)(2,1)S(1)}, u32[]{:S(2)}, u32[]{:S(2)}) collective-permute-start(bf16[6,2,1,128]{3,2,1,0:T(2,128)(2,1)S(1)} %get-tuple-element.63), channel_id=1, source_target_pairs={{0,1},{1,2},{2,3},{3,4},{4,5},{5,6},{6,7},{7,8},{8,9},{9,10},{10,1... | collective-permute-start | bytes 9224 | tf_op jit(solution)/shard_map/ppermute | solution.py:28
  203.6 8.5 %collective-permute-start.9 = (f32[3,2,128,128]{3,2,1,0:T(8,128)S(1)}, f32[3,2,128,128]{3,2,1,0:T(8,128)S(1)}, u32[]{:S(2)}, u32[]{:S(2)}) collective-permute-start(f32[3,2,128,128]{3,2,1,0:T(8,128)S(1)} %slice.2023), channel_id=1, source_target_pairs={{16,0},{32,16},{48,32},{64,48},{80,64},{96,80},{112,96},{128,112},... | collective-permute-start | bytes 1179656 | tf_op jit(solution)/shard_map/ppermute | solution.py:20
  212.7 11.8 %collective-permute-start.10 = (f32[3,2,128,128]{3,2,1,0:T(8,128)S(1)}, f32[3,2,128,128]{3,2,1,0:T(8,128)S(1)}, u32[]{:S(2)}, u32[]{:S(2)}) collective-permute-start(f32[3,2,128,128]{3,2,1,0:T(8,128)S(1)} %pad_maximum_fusion.2), channel_id=1, source_target_pairs={{0,16},{16,32},{32,48},{48,64},{64,80},{80,96},{96,112},{112,128},... | collective-permute-start | bytes 1179656 | tf_op jit(solution)/shard_map/ppermute | solution.py:20
  (37 other events, 112.8 us)
where the time goes:
time: 228 us; the launch traced here: 226 us
  starting transfers between devices  60.6 us (27%)
  waiting for transfers between devices  49.8 us (22%)
  between operations  36 us (16%)
  other arithmetic  35.7 us (16%)
  matrix products  34.2 us (15%)
  local copies, waits for them, and re-layouts  9.61 us (4%)
    ppermute x7, waiting for transfers between devices, from_behind(): lax.ppermute(value, axis, [(source, source + steps) for source in range(i...  49.8 us
    ppermute x3, starting transfers between devices, with_halo(): lax.ppermute(lax.slice_in_dim(block, block.shape[dim] - width, None, axis...  35 us
    ppermute x7, starting transfers between devices, from_behind(): lax.ppermute(value, axis, [(source, source + steps) for source in range(i...  17.8 us
    convert_element_type x36, other arithmetic, kernel_tables(): return (smooth.astype(jnp.bfloat16), slopes.astype(jnp.bfloat16))  14.7 us
    dot_general x18, matrix products, pair_cache(): lax.dot_general(picture, col_tables, (((1,), (1,)), ((), ())), preferred_...  13.5 us
    dot_general x6, matrix products, own_pool(): jnp.dot(smooth, halfway, preferred_element_type=jnp.float32)  9.28 us
    ppermute x3, starting transfers between devices, with_halo(): lax.ppermute(lax.slice_in_dim(block, 0, width, axis=dim), axis, backward)  7.83 us
    reduce_sum x37, other arithmetic, kernel_tables(): smooth = kernel / jnp.sum(kernel, axis=1, keepdims=True)  7.71 us
  transfers between devices with their start and end apart: 13, of which 5 were waited for; matrix products, arithmetic and copies ran while one was open for 33% of the time, Pallas kernels for 0%

commit v1 on v0

v1 whole, which is shorter than its diff:
```python
import functools

import jax
import jax.numpy as jnp
from jax import lax
from jax.experimental import pallas as pl
from jax.experimental.pallas import tpu as pltpu
from jax.sharding import PartitionSpec as P

PIXELS = 512
GRID = 128
SKIPS = 3
ITERS = 3
RES = 6
FIELDS = 2 * RES
PAD = 8
BLOCK = 16
F32, BF16 = jnp.float32, jnp.bfloat16
MESH = pl.DeviceIdType.MESH

SEGS = ((0, 16), (112, 16), (16, 32), (48, 32), (80, 32))
CROSS = ((0, 1), (0, 2), (0, 3), (1, 2), (1, 3), (2, 3))
LOCAL = ((1, 1), (2, 1), (2, 2), (3, 1), (3, 2), (3, 3), (4, 1), (4, 2), (4, 3), (5, 1), (5, 2), (5, 3))

kernel_sigma = 2.0
force_step = 0.5
elastic_step = 0.1


def bell(spread, axis):
    peak = jnp.exp(-spread * spread / (2.0 * kernel_sigma * kernel_sigma))
    smooth = peak / jnp.sum(peak, axis=axis, keepdims=True)
    slopes = smooth * spread / (kernel_sigma * kernel_sigma)
    return smooth.astype(BF16), slopes.astype(BF16)


def kernel(disp, images, offsets, weights, stiffness, out, img, rows_t, cols_t, cache, crecv, pool, precv,
           pad_a, pad_b, pad_c, fin, part, usend, uprev, unext, rimsend, rimrecv, meta_v, meta_r, meta_s,
           img_sem, loc_sem, u_ssem, u_rsem, c_ssem, c_rsem, q_sem, rim_ssem, rim_rsem, m_sem):
    me, col = lax.axis_index("sec"), lax.axis_index("tile")
    has_prev, has_next = me > 0, me < lax.axis_size("sec") - 1
    has_up, has_down = col > 0, col < lax.axis_size("tile") - 1
    pads = (pad_a, pad_b, pad_c)

    barrier = pltpu.get_barrier_semaphore()
    sides = ((has_prev, {"sec": me - 1}), (has_next, {"sec": me + 1}), (has_up, {"tile": col - 1}), (has_down, {"tile": col + 1}))
    for there, target in sides:
        @pl.when(there)
        def _():
            pl.semaphore_signal(barrier, inc=1, device_id=target, device_id_type=MESH)

    def fetch(section):
        return pltpu.make_async_copy(images.at[section], img.at[section], img_sem.at[section])

    load_u = pltpu.make_async_copy(disp, pad_a.at[:, pl.ds(PAD, GRID), :], loc_sem.at[0])
    load_u.start()
    for section in (3, 4, 5, 0, 1, 2):
        fetch(section).start()

    spacing = PIXELS // GRID

    def table(offset, carry):
        shift = (spacing - 1) / 2.0 + offset.astype(F32)
        cell = lax.broadcasted_iota(jnp.int32, (GRID, PIXELS), 0).astype(F32)
        pixel = lax.broadcasted_iota(jnp.int32, (GRID, PIXELS), 1).astype(F32)
        smooth, slopes = bell(pixel - (spacing * cell + shift), 1)
        rows_t[offset, 0:GRID, :] = smooth
        rows_t[offset, GRID:2 * GRID, :] = slopes
        cell = lax.broadcasted_iota(jnp.int32, (PIXELS, GRID), 1).astype(F32)
        pixel = lax.broadcasted_iota(jnp.int32, (PIXELS, GRID), 0).astype(F32)
        smooth, slopes = bell(pixel - (spacing * cell + shift), 0)
        cols_t[offset, :, 0:GRID] = smooth
        cols_t[offset, :, GRID:2 * GRID] = slopes
        return carry

    lax.fori_loop(0, SKIPS + 1, table, 0)

    lane = lax.broadcasted_iota(jnp.int32, (8, 128), 1)
    facts = jnp.zeros((8, 128), jnp.int32)
    for section in range(SKIPS):
        for stride in range(SKIPS):
            base = (section * SKIPS + stride) * 3
            facts = jnp.where(lane == base, offsets[(section + SKIPS), stride, 0], facts)
            facts = jnp.where(lane == base + 1, offsets[(section + SKIPS), stride, 1], facts)
            facts = jnp.where(lane == base + 2, weights[(section + SKIPS), stride], facts)
    meta_v[...] = facts

    load_u.wait()

    def halve(block, carry):
        at = pl.ds(pl.multiple_of(block * BLOCK, BLOCK), BLOCK)
        from_pad = pl.ds(pl.multiple_of(block * BLOCK + PAD, PAD), BLOCK)
        for field in range(FIELDS):
            usend[0, field, at, :] = pad_a[field, from_pad, :].astype(BF16)
        return carry

    lax.fori_loop(0, GRID // BLOCK, halve, 0)

    zero_row = jnp.zeros((PAD, GRID), F32)
    for pad in pads:
        for field in range(FIELDS):
            pad[field, 0:PAD, :] = zero_row
            pad[field, PAD + GRID:, :] = zero_row

    def keep_rims(step, source, base):
        for field in range(FIELDS):
            rimsend[step, 0, field:field + 1, :] = source[field, base:base + 1, :]
            rimsend[step, 1, field:field + 1, :] = source[field, base + GRID - 1:base + GRID, :]

    rimsend[...] = jnp.zeros_like(rimsend)
    keep_rims(0, pad_a, PAD)

    @pl.when(jnp.logical_not(has_prev))
    def _():
        meta_r[...] = jnp.zeros_like(meta_r)
        uprev[...] = jnp.zeros_like(uprev)
        precv[...] = jnp.zeros_like(precv)

    @pl.when(jnp.logical_not(has_next))
    def _():
        unext[...] = jnp.zeros_like(unext)
        crecv[...] = jnp.zeros_like(crecv)

    @pl.when(jnp.logical_not(has_up))
    def _():
        rimrecv[:, 1] = jnp.zeros((ITERS, 16, GRID), F32)

    @pl.when(jnp.logical_not(has_down))
    def _():
        rimrecv[:, 0] = jnp.zeros((ITERS, 16, GRID), F32)

    pl.semaphore_wait(barrier, sum(there.astype(jnp.int32) for there, _ in sides))

    half = SKIPS * 2

    def facts_copy():
        return pltpu.make_async_remote_copy(
            src_ref=meta_v, dst_ref=meta_r, send_sem=m_sem.at[0], recv_sem=m_sem.at[1], device_id={"sec": me + 1}, device_id_type=MESH)

    def u_back(step, seg):
        start, size = SEGS[seg]
        at = pl.ds(start, size)
        return pltpu.make_async_remote_copy(
            src_ref=usend.at[step, pl.ds(0, half), at, :], dst_ref=unext.at[step, :, at, :], send_sem=u_ssem.at[step, 0, seg],
            recv_sem=u_rsem.at[step, 0, seg], device_id={"sec": me - 1}, device_id_type=MESH)

    def u_forth(step, seg):
        start, size = SEGS[seg]
        at = pl.ds(start, size)
        return pltpu.make_async_remote_copy(
            src_ref=usend.at[step, pl.ds(half, half), at, :], dst_ref=uprev.at[step, :, at, :], send_sem=u_ssem.at[step, 1, seg],
            recv_sem=u_rsem.at[step, 1, seg], device_id={"sec": me + 1}, device_id_type=MESH)

    def c_back(pair, seg):
        start, size = SEGS[seg]
        at = pl.ds(start, size)
        return pltpu.make_async_remote_copy(
            src_ref=cache.at[pair, :, at, :], dst_ref=crecv.at[pair, :, at, :], send_sem=c_ssem.at[pair, seg],
            recv_sem=c_rsem.at[pair, seg], device_id={"sec": me - 1}, device_id_type=MESH)

    def q_forth():
        return pltpu.make_async_remote_copy(
            src_ref=pool.at[pl.ds(SKIPS, SKIPS)], dst_ref=precv, send_sem=q_sem.at[0], recv_sem=q_sem.at[1],
            device_id={"sec": me + 1}, device_id_type=MESH)

    def rim_copy(step, side):
        target = col - 1 if side == 0 else col + 1
        return pltpu.make_async_remote_copy(
            src_ref=rimsend.at[step, side], dst_ref=rimrecv.at[step, side], send_sem=rim_ssem.at[step, side],
            recv_sem=rim_rsem.at[step, side], device_id={"tile": target}, device_id_type=MESH)

    def send_rims(step):
        @pl.when(has_up)
        def _():
            rim_copy(step, 0).start()

        @pl.when(has_down)
        def _():
            rim_copy(step, 1).start()

    @pl.when(has_next)
    def _():
        facts_copy().start()
        for seg in range(len(SEGS)):
            u_forth(0, seg).start()

    @pl.when(has_prev)
    def _():
        for seg in range(len(SEGS)):
            u_back(0, seg).start()

    send_rims(0)

    def own_pool(section):
        halfway = jnp.dot(img[section], cols_t[0, :, 0:GRID], preferred_element_type=F32).astype(BF16)
        pool[section] = jnp.dot(rows_t[0, 0:GRID, :], halfway, preferred_element_type=F32).astype(BF16)

    def pair_cache(slot, section, off_r, off_c):
        halfway = jnp.dot(img[section], cols_t[off_c], preferred_element_type=F32).astype(BF16)
        pooled = jnp.dot(rows_t[off_r], halfway, preferred_element_type=F32).astype(BF16)
        cache[slot, 0] = pooled[:GRID, :GRID]
        cache[slot, 1] = pooled[GRID:, :GRID]
        cache[slot, 2] = pooled[:GRID, GRID:]

    def own_step(section, carry):
        fetch(section).wait()
        own_pool(section)
        return carry

    lax.fori_loop(SKIPS, RES, own_step, 0)

    @pl.when(has_next)
    def _():
        q_forth().start()

    for section in range(SKIPS):
        fetch(section).wait()

    @pl.when(has_prev)
    def _():
        facts_copy().wait_recv()

    to_scalars = pltpu.make_async_copy(meta_r, meta_s, loc_sem.at[1])
    to_scalars.start()
    to_scalars.wait()

    def cross_step(slot, carry):
        first, second = (slot >= 3).astype(jnp.int32), (slot >= 5).astype(jnp.int32)
        section = first + second
        stride = slot + 1 - 2 * first - second
        base = ((section - stride + SKIPS) * SKIPS + stride - 1) * 3
        pair_cache(slot, section, meta_s[0, base], meta_s[0, base + 1])

        @pl.when(has_prev)
        def _():
            c_back(slot, 0).start()
            c_back(slot, 1).start()

        return carry

    lax.fori_loop(0, len(CROSS), cross_step, 0)

    @pl.when(has_prev)
    def _():
        for seg in range(2, len(SEGS)):
            for pair in range(len(CROSS)):
                c_back(pair, seg).start()

    def own_first(section, carry):
        own_pool(section)
        return carry

    lax.fori_loop(0, SKIPS, own_first, 0)

    def local_step(step, carry):
        late = (step >= 3).astype(jnp.int32)
        section = late * (3 + (step - 3) // 3) + (1 - late) * (1 + (step >= 1).astype(jnp.int32))
        stride = late * ((step - 3) % 3 + 1) + (1 - late) * (1 + (step >= 2).astype(jnp.int32))
        earlier = section - stride
        pair_cache(len(CROSS) + step, section, offsets[earlier, stride - 1, 0], offsets[earlier, stride - 1, 1])
        return carry

    lax.fori_loop(0, len(LOCAL), local_step, 0)

    gain = [[force_step * weights[s, k - 1].astype(F32) for k in range(1, SKIPS + 1)] for s in range(RES)]
    onward = has_next.astype(F32)
    stiff = [elastic_step * stiffness[s] for s in range(RES)]

    def pull(pair_ref, slot, at, earlier_pool, row_gap, col_gap, scale):
        steep = (pair_ref[slot, 1, at, :].astype(F32), pair_ref[slot, 2, at, :].astype(F32))
        miss = pair_ref[slot, 0, at, :].astype(F32) - earlier_pool + steep[0] * row_gap + steep[1] * col_gap
        weighted = scale * (miss / (1.0 + miss * miss))
        return weighted * steep[0], weighted * steep[1]

    def local_pass(pad):
        def block_step(block, carry):
            start = block * BLOCK
            at = pl.ds(pl.multiple_of(start, BLOCK), BLOCK)
            mid = pl.ds(pl.multiple_of(start + PAD, PAD), BLOCK)
            above = pl.ds(start + PAD - 1, BLOCK)
            below = pl.ds(start + PAD + 1, BLOCK)
            edge = lax.broadcasted_iota(jnp.int32, (BLOCK, GRID), 1)
            total = []
            for field in range(FIELDS):
                here = pad[field, mid, :]
                left = jnp.where(edge == 0, 0.0, pltpu.roll(here, 1, 1))
                right = jnp.where(edge == GRID - 1, 0.0, pltpu.roll(here, GRID - 1, 1))
                beside = pad[field, above, :] + pad[field, below, :] + left + right
                total.append(here - stiff[field // 2] * (4.0 * here - beside))
            for index, (later, stride) in enumerate(LOCAL):
                earlier = later - stride
                gaps = [pad[2 * later + c, mid, :] - pad[2 * earlier + c, mid, :] for c in range(2)]
                pulled = pull(cache, len(CROSS) + index, at, pool[earlier, at, :].astype(F32), gaps[0], gaps[1], gain[earlier][stride - 1])
                for c in range(2):
                    total[2 * earlier + c] += pulled[c]
                    total[2 * later + c] -= pulled[c]
            for field in range(FIELDS):
                part[field, at, :] = total[field]
            return carry

        lax.fori_loop(0, GRID // BLOCK, block_step, 0)

    cross_gain = []
    for later, stride in CROSS:
        base = ((later - stride + SKIPS) * SKIPS + stride - 1) * 3
        cross_gain.append(force_step * meta_s[0, base + 2].astype(F32))

    def cross_pass(step, pad, seg):
        first, size = SEGS[seg]

        def block_step(index, carry):
            start = first + index * BLOCK
            at = pl.ds(pl.multiple_of(start, BLOCK), BLOCK)
            mid = pl.ds(pl.multiple_of(start + PAD, PAD), BLOCK)
            total = [part[field, at, :] for field in range(FIELDS)]
            for slot, (later, stride) in enumerate(CROSS):
                earlier = later - stride + SKIPS
                gaps = [pad[2 * later + c, mid, :] - uprev[step, 2 * earlier + c, at, :].astype(F32) for c in range(2)]
                pulled = pull(cache, slot, at, precv[earlier, at, :].astype(F32), gaps[0], gaps[1], cross_gain[slot])
                for c in range(2):
                    total[2 * later + c] -= pulled[c]
            for slot, (later, stride) in enumerate(CROSS):
                earlier = later - stride + RES
                gaps = [unext[step, 2 * later + c, at, :].astype(F32) - pad[2 * earlier + c, mid, :] for c in range(2)]
                pulled = pull(crecv, slot, at, pool[earlier, at, :].astype(F32), gaps[0], gaps[1], onward * gain[earlier][stride - 1])
                for c in range(2):
                    total[2 * earlier + c] += pulled[c]
            for field in range(FIELDS):
                if step + 1 < ITERS:
                    pads[step + 1][field, mid, :] = total[field]
                    usend[step + 1, field, at, :] = total[field].astype(BF16)
                else:
                    fin[field, at, :] = total[field]
            return carry

        lax.fori_loop(0, size // BLOCK, block_step, 0)

    def store(seg):
        start, size = SEGS[seg]
        return pltpu.make_async_copy(fin.at[:, pl.ds(start, size), :], out.at[:, pl.ds(start, size), :], loc_sem.at[2 + seg])

    for step in range(ITERS):
        pad = pads[step]
        local_pass(pad)
        if step == 0:
            @pl.when(has_prev)
            def _():
                q_forth().wait_recv()

        order = (0, 1, 2, 3, 4) if step == 0 else (2, 3, 4, 0, 1)
        for seg in order:
            @pl.when(has_prev)
            def _():
                u_forth(step, seg).wait_recv()

            @pl.when(has_next)
            def _():
                u_back(step, seg).wait_recv()
                if step == 0:
                    for pair in range(len(CROSS)):
                        c_back(pair, seg).wait_recv()

            if seg == 0:
                @pl.when(has_up)
                def _():
                    rim_copy(step, 1).wait_recv()

                for field in range(FIELDS):
                    part[field, 0:1, :] = part[field, 0:1, :] + stiff[field // 2] * rimrecv[step, 1, field:field + 1, :]
            if seg == 1:
                @pl.when(has_down)
                def _():
                    rim_copy(step, 0).wait_recv()

                for field in range(FIELDS):
                    part[field, GRID - 1:GRID, :] = part[field, GRID - 1:GRID, :] + stiff[field // 2] * rimrecv[step, 0, field:field + 1, :]
            cross_pass(step, pad, seg)
            if step + 1 < ITERS:
                @pl.when(has_prev)
                def _():
                    u_back(step + 1, seg).start()

                @pl.when(has_next)
                def _():
                    u_forth(step + 1, seg).start()

                if seg == 1:
                    keep_rims(step + 1, pads[step + 1], PAD)
                    send_rims(step + 1)
            else:
                store(seg).start()

    for seg in range(len(SEGS)):
        store(seg).wait()

    @pl.when(has_prev)
    def _():
        for seg in range(len(SEGS)):
            for step in range(ITERS):
                u_back(step, seg).wait_send()
            for pair in range(len(CROSS)):
                c_back(pair, seg).wait_send()

    @pl.when(has_next)
    def _():
        facts_copy().wait_send()
        q_forth().wait_send()
        for seg in range(len(SEGS)):
            for step in range(ITERS):
                u_forth(step, seg).wait_send()

    for step in range(ITERS):
        @pl.when(has_up)
        def _():
            rim_copy(step, 0).wait_send()

        @pl.when(has_down)
        def _():
            rim_copy(step, 1).wait_send()


def local(images, displacement, offsets, weights, stiffness):
    anywhere = pl.BlockSpec(memory_space=pl.ANY)
    scalars = pl.BlockSpec(memory_space=pltpu.SMEM)
    dma, vmem = pltpu.SemaphoreType.DMA, pltpu.VMEM
    segs, cross = len(SEGS), len(CROSS)
    moved = pl.pallas_call(
        kernel,
        out_shape=jax.ShapeDtypeStruct((FIELDS, GRID, GRID), F32),
        in_specs=[anywhere, anywhere, scalars, scalars, scalars],
        out_specs=anywhere,
        scratch_shapes=[
            vmem((RES, PIXELS, PIXELS), BF16),
            vmem((SKIPS + 1, 2 * GRID, PIXELS), BF16),
            vmem((SKIPS + 1, PIXELS, 2 * GRID), BF16),
            vmem((cross + len(LOCAL), 3, GRID, GRID), BF16),
            vmem((cross, 3, GRID, GRID), BF16),
            vmem((RES, GRID, GRID), BF16),
            vmem((SKIPS, GRID, GRID), BF16),
            vmem((FIELDS, GRID + 2 * PAD, GRID), F32),
            vmem((FIELDS, GRID + 2 * PAD, GRID), F32),
            vmem((FIELDS, GRID + 2 * PAD, GRID), F32),
            vmem((FIELDS, GRID, GRID), F32),
            vmem((FIELDS, GRID, GRID), F32),
            vmem((ITERS, FIELDS, GRID, GRID), BF16),
            vmem((ITERS, 2 * SKIPS, GRID, GRID), BF16),
            vmem((ITERS, 2 * SKIPS, GRID, GRID), BF16),
            vmem((ITERS, 2, 16, GRID), F32),
            vmem((ITERS, 2, 16, GRID), F32),
            vmem((8, 128), jnp.int32),
            vmem((8, 128), jnp.int32),
            pltpu.SMEM((8, 128), jnp.int32),
            dma((RES,)),
            dma((2 + segs,)),
            dma((ITERS, 2, segs)),
            dma((ITERS, 2, segs)),
            dma((cross, segs)),
            dma((cross, segs)),
            dma((2,)),
            dma((ITERS, 2)),
            dma((ITERS, 2)),
            dma((2,)),
        ],
        compiler_params=pltpu.CompilerParams(collective_id=0, has_side_effects=True, vmem_limit_bytes=67_000_000),
    )(displacement.reshape(FIELDS, GRID, GRID), images, offsets, weights, stiffness)
    return moved.reshape(RES, 2, GRID, GRID)


def solution(mesh):
    placed = (
        P("sec", "tile", None),
        P("sec", None, "tile", None),
        P("sec", None, None),
        P("sec", None),
        P("sec"),
    )
    return jax.shard_map(
        local, mesh=mesh, in_specs=placed, out_specs=P("sec", None, "tile", None), check_vma=False
    )
```

time: 228 us -> 56.1 us (0.25)
  the two profiles are of different devices: /device:TPU:153 before, /device:TPU:56 now
where the time goes in v1:
time: 56.1 us; the launch traced here: 55.8 us
  Pallas kernels  51 us (91%)
  local copies, waits for them, and re-layouts  4.79 us (9%)
    pallas_call x1, Pallas kernels, local(): pl.pallas_call(kernel, out_shape=jax.ShapeDtypeStruct((FIELDS, GRID, GRID...  51 us
    unnamed x3, local copies, waits for them, and re-layouts  4.79 us

profile of v1, /device:TPU:56, one launch (start us, length us, event | category | flops | bytes accessed | tf_op | source)
XLA Modules:
  0.0 55.8 jit_solution(10116087182369005912)
XLA Ops:
  0.0 1.3 %copy.7.weights = s32[6,3]{1,0:T(8,128)} copy(s32[6,3]{0,1:T(4,128)} %param.8) | data formatting | bytes 144 | tf_op args[3]
  1.4 1.4 %copy.6.offsets = s32[6,3,2]{2,1,0:T(4,128)} copy(s32[6,3,2]{0,2,1:T(2,128)} %param.7) | data formatting | bytes 288 | tf_op args[2]
  2.7 51.0 %shard_map.55 = f32[12,128,128]{2,1,0:T(8,128)} custom-call(f32[12,128,128]{2,1,0:T(8,128)} %bitcast.3, bf16[6,512,512]{2,1,0:T(8,128)(2,1)} %images.1, s32[6,3,2]{2,1,0:T(4,128)} %copy.6.offsets, s32[6,3]{1,0:T(8,128)} %copy.7.weights, f32[6]{0:T(128)} %stiffness.1), custom_call_target="tpu_custom_call" | custom-call | tf_op jit(solution)/shard_map/pallas_call | solution.py:427
  53.7 2.1 %copy.9 = f32[6,2,128,128]{3,2,1,0:T(8,128)} copy(f32[6,2,128,128]{3,2,1,0:T(8,128)} %bitcast.2) | data formatting | bytes 1572864

commit v2 on v1

v2 whole, which is shorter than its diff:
```python
import jax
import jax.numpy as jnp
from jax import lax
from jax.experimental import pallas as pl
from jax.experimental.pallas import tpu as pltpu
from jax.sharding import PartitionSpec as P

PIXELS = 512
HALF = PIXELS // 2
GRID = 128
SKIPS = 3
ITERS = 3
RES = 6
FIELDS = 2 * RES
EDGE = 2 * SKIPS
PAD = 8
BLOCK = 16
REACH = 72
MEET = 2 * REACH - GRID
F32, BF16 = jnp.float32, jnp.bfloat16
MESH = pl.DeviceIdType.MESH

SEGS = ((0, 16), (112, 16), (16, 32), (48, 32), (80, 32))
CROSS = ((0, 1), (0, 2), (0, 3), (1, 2), (1, 3), (2, 3))
LOCAL = ((1, 1), (2, 1), (2, 2), (3, 1), (3, 2), (3, 3), (4, 1), (4, 2), (4, 3), (5, 1), (5, 2), (5, 3))

kernel_sigma = 2.0
force_step = 0.5
elastic_step = 0.1


def dot_rows(left, right):
    return lax.dot_general(left, right, (((1,), (1,)), ((), ())), preferred_element_type=F32)


def meet(top, bottom):
    own = REACH - MEET
    return jnp.concatenate([top[:own], top[own:] + bottom[:MEET], bottom[MEET:]], axis=0)


def kernel(disp, images, offsets_hbm, weights_hbm, stiffness_hbm, out, img, first_t, last_t, cache, pool, precv,
           pad_a, pad_b, pad_c, fin, cross_own, usend, uprev, fsend, frecv, rimsend, rimrecv, meta_v, meta_r, meta_s,
           offsets, weights, stiffness, img_sem, loc_sem, u_ssem, u_rsem, f_ssem, f_rsem, q_ssem, q_rsem, rim_ssem, rim_rsem, m_sem):
    me, col = lax.axis_index("sec"), lax.axis_index("tile")
    has_prev, has_next = me > 0, me < lax.axis_size("sec") - 1
    has_up, has_down = col > 0, col < lax.axis_size("tile") - 1
    before, after = {"sec": me - 1}, {"sec": me + 1}
    pads = (pad_a, pad_b, pad_c)
    segments = range(len(SEGS))

    barrier = pltpu.get_barrier_semaphore()
    sides = ((has_prev, before), (has_next, after), (has_up, {"tile": col - 1}), (has_down, {"tile": col + 1}))
    for there, target in sides:
        @pl.when(there)
        def _():
            pl.semaphore_signal(barrier, inc=1, device_id=target, device_id_type=MESH)

    scalars = [pltpu.make_async_copy(src, dst, loc_sem.at[place]) for place, (src, dst) in enumerate(
        ((offsets_hbm, offsets), (weights_hbm, weights), (stiffness_hbm, stiffness)))]
    for copy in scalars:
        copy.start()
    load_u = pltpu.make_async_copy(disp, pad_a.at[:, pl.ds(PAD, GRID), :], loc_sem.at[3])
    load_u.start()

    def fetch(section):
        return pltpu.make_async_copy(images.at[section], img.at[section], img_sem.at[section])

    for section in (3, 4, 5, 0, 1, 2):
        fetch(section).start()

    spacing = PIXELS // GRID

    def table(offset, carry):
        shift = (spacing - 1) / 2.0 + offset.astype(F32)
        cell = lax.broadcasted_iota(jnp.int32, (REACH, HALF), 0).astype(F32)
        pixel = lax.broadcasted_iota(jnp.int32, (REACH, HALF), 1).astype(F32)
        spread, peak, mass = [], [], []
        for low_cell, low_pixel in ((0, 0), (GRID - REACH, HALF)):
            gap = (pixel + low_pixel) - (spacing * (cell + low_cell) + shift)
            spread.append(gap)
            peak.append(jnp.exp(-gap * gap / (2.0 * kernel_sigma * kernel_sigma)))
            mass.append(jnp.sum(peak[-1], axis=1, keepdims=True))
        own = REACH - MEET
        shared = mass[0][own:] + mass[1][:MEET]
        mass = (jnp.concatenate([mass[0][:own], shared], axis=0), jnp.concatenate([shared, mass[1][MEET:]], axis=0))
        for half, ref in enumerate((first_t, last_t)):
            smooth = peak[half] / mass[half]
            ref[offset, 0:REACH, :] = smooth.astype(BF16)
            ref[offset, REACH:2 * REACH, :] = (smooth * spread[half] / (kernel_sigma * kernel_sigma)).astype(BF16)
        return carry

    for copy in scalars:
        copy.wait()

    lane = lax.broadcasted_iota(jnp.int32, (8, 128), 1)
    facts = jnp.zeros((8, 128), jnp.int32)
    for section in range(SKIPS):
        for stride in range(SKIPS):
            base = (section * SKIPS + stride) * 3
            facts = jnp.where(lane == base, offsets[stride, 0, section + SKIPS], facts)
            facts = jnp.where(lane == base + 1, offsets[stride, 1, section + SKIPS], facts)
            facts = jnp.where(lane == base + 2, weights[stride, section + SKIPS], facts)
    meta_v[...] = facts
    rimsend[...] = jnp.zeros_like(rimsend)

    @pl.when(jnp.logical_not(has_prev))
    def _():
        meta_r[...] = jnp.zeros_like(meta_r)
        uprev[...] = jnp.zeros_like(uprev)
        precv[...] = jnp.zeros_like(precv)

    @pl.when(jnp.logical_not(has_next))
    def _():
        frecv[...] = jnp.zeros_like(frecv)

    @pl.when(jnp.logical_not(has_up))
    def _():
        rimrecv[:, 1] = jnp.zeros((ITERS, 16, GRID), F32)

    @pl.when(jnp.logical_not(has_down))
    def _():
        rimrecv[:, 0] = jnp.zeros((ITERS, 16, GRID), F32)

    load_u.wait()

    def halve(block, carry):
        at = pl.ds(pl.multiple_of(block * BLOCK, BLOCK), BLOCK)
        from_pad = pl.ds(pl.multiple_of(block * BLOCK + PAD, PAD), BLOCK)
        for field in range(EDGE):
            usend[0, field, at, :] = pad_a[EDGE + field, from_pad, :].astype(BF16)
        return carry

    lax.fori_loop(0, GRID // BLOCK, halve, 0)

    def keep_rims(step, source):
        for field in range(FIELDS):
            rimsend[step, 0, field:field + 1, :] = source[field, PAD:PAD + 1, :]
            rimsend[step, 1, field:field + 1, :] = source[field, PAD + GRID - 1:PAD + GRID, :]

    keep_rims(0, pad_a)


    pl.semaphore_wait(barrier, sum(there.astype(jnp.int32) for there, _ in sides))


    def remote(src, dst, send_sem, recv_sem, target):
        return pltpu.make_async_remote_copy(
            src_ref=src, dst_ref=dst, send_sem=send_sem, recv_sem=recv_sem, device_id=target, device_id_type=MESH)

    def facts_copy():
        return remote(meta_v, meta_r, m_sem.at[0], m_sem.at[1], after)

    def rows_of(seg):
        start, size = SEGS[seg]
        return pl.ds(start, size)

    def u_forth(step, seg):
        at = rows_of(seg)
        return remote(usend.at[step, :, at, :], uprev.at[step, :, at, :], u_ssem.at[step, seg], u_rsem.at[step, seg], after)

    def f_back(step, seg):
        at = rows_of(seg)
        return remote(fsend.at[step, :, at, :], frecv.at[step, :, at, :], f_ssem.at[step, seg], f_rsem.at[step, seg], before)

    def q_forth(index):
        return remote(pool.at[index + SKIPS], precv.at[index], q_ssem.at[index], q_rsem.at[index], after)

    def rim_copy(step, side):
        target = {"tile": col - 1 if side == 0 else col + 1}
        return remote(rimsend.at[step, side], rimrecv.at[step, side], rim_ssem.at[step, side], rim_rsem.at[step, side], target)

    def send_rims(step):
        @pl.when(has_up)
        def _():
            rim_copy(step, 0).start()

        @pl.when(has_down)
        def _():
            rim_copy(step, 1).start()

    @pl.when(has_next)
    def _():
        facts_copy().start()
        for seg in segments:
            u_forth(0, seg).start()

    send_rims(0)


    lax.fori_loop(0, SKIPS + 1, table, 0)
    zero_row = jnp.zeros((PAD, GRID), F32)
    for pad in pads:
        for field in range(FIELDS):
            pad[field, 0:PAD, :] = zero_row
            pad[field, PAD + GRID:, :] = zero_row

    def columns(section, first, last, count):
        parts = []
        for low in (0, HALF):
            top = dot_rows(first, img[section, low:low + HALF, 0:HALF])
            bottom = dot_rows(last, img[section, low:low + HALF, HALF:])
            parts.append(jnp.concatenate([
                meet(top[REACH * one:REACH * (one + 1)], bottom[REACH * one:REACH * (one + 1)]) for one in range(count)], axis=0).astype(BF16))
        return parts

    def own_pool(section):
        parts = columns(section, first_t[0, 0:REACH, :], last_t[0, 0:REACH, :], 1)
        pool[section] = meet(dot_rows(first_t[0, 0:REACH, :], parts[0]), dot_rows(last_t[0, 0:REACH, :], parts[1])).astype(BF16)

    def pair_cache(slot, section, off_r, off_c):
        parts = columns(section, first_t[off_c], last_t[off_c], 2)
        top, bottom = dot_rows(first_t[off_r], parts[0]), dot_rows(last_t[off_r], parts[1])
        smooth = meet(top[:REACH], bottom[:REACH]).astype(BF16)
        cache[slot, 0] = smooth[:, :GRID]
        cache[slot, 1] = meet(top[REACH:, :GRID], bottom[REACH:, :GRID]).astype(BF16)
        cache[slot, 2] = smooth[:, GRID:]


    def own_step(section, carry):
        fetch(section).wait()
        own_pool(section)

        @pl.when(has_next)
        def _():
            q_forth(section - SKIPS).start()

        return carry

    lax.fori_loop(SKIPS, RES, own_step, 0)

    for section in range(SKIPS):
        fetch(section).wait()


    @pl.when(has_prev)
    def _():
        facts_copy().wait_recv()

    to_scalars = pltpu.make_async_copy(meta_r, meta_s, loc_sem.at[4])
    to_scalars.start()
    to_scalars.wait()


    def cross_step(slot, carry):
        first, second = (slot >= 3).astype(jnp.int32), (slot >= 5).astype(jnp.int32)
        section = first + second
        stride = slot + 1 - 2 * first - second
        base = ((section - stride + SKIPS) * SKIPS + stride - 1) * 3
        pair_cache(slot, section, meta_s[0, base], meta_s[0, base + 1])
        return carry

    lax.fori_loop(0, len(CROSS), cross_step, 0)

    gain = [[force_step * weights[k - 1, s].astype(F32) for k in range(1, SKIPS + 1)] for s in range(RES)]
    stiff = [elastic_step * stiffness[s] for s in range(RES)]
    cross_gain = []
    for later, stride in CROSS:
        base = ((later - stride + SKIPS) * SKIPS + stride - 1) * 3
        cross_gain.append(force_step * meta_s[0, base + 2].astype(F32))

    def pull(slot, at, earlier_pool, row_gap, col_gap, scale):
        steep = (cache[slot, 1, at, :].astype(F32), cache[slot, 2, at, :].astype(F32))
        miss = cache[slot, 0, at, :].astype(F32) - earlier_pool + steep[0] * row_gap + steep[1] * col_gap
        weighted = scale * (miss / (1.0 + miss * miss))
        return weighted * steep[0], weighted * steep[1]

    def over(seg, body):
        start, size = SEGS[seg]

        def block_step(index, carry):
            low = start + index * BLOCK
            body(low, pl.ds(pl.multiple_of(low, BLOCK), BLOCK), pl.ds(pl.multiple_of(low + PAD, PAD), BLOCK))
            return carry

        lax.fori_loop(0, size // BLOCK, block_step, 0)

    def cross_pass(step, seg):
        pad = pads[step]

        def body(low, at, mid):
            own, back = [None] * EDGE, [None] * EDGE
            for slot, (later, stride) in enumerate(CROSS):
                earlier = later - stride + SKIPS
                gaps = [pad[2 * later + c, mid, :] - uprev[step, 2 * earlier + c, at, :].astype(F32) for c in range(2)]
                pulled = pull(slot, at, precv[earlier, at, :].astype(F32), gaps[0], gaps[1], cross_gain[slot])
                for c in range(2):
                    here, there = 2 * later + c, 2 * earlier + c
                    own[here] = pulled[c] if own[here] is None else own[here] + pulled[c]
                    back[there] = pulled[c] if back[there] is None else back[there] + pulled[c]
            for field in range(EDGE):
                cross_own[field, at, :] = own[field]
                fsend[step, field, at, :] = back[field].astype(BF16)

        over(seg, body)

    def cross_turn(step, seg):
        @pl.when(has_prev)
        def _():
            u_forth(step, seg).wait_recv()

        cross_pass(step, seg)

        @pl.when(has_prev)
        def _():
            f_back(step, seg).start()

    def goal(step):
        return (pads[step + 1], PAD) if step + 1 < ITERS else (fin, 0)

    def local_pass(step, seg):
        pad, (target, base) = pads[step], goal(step)

        def body(low, at, mid):
            put = pl.ds(pl.multiple_of(low + base, PAD), BLOCK)
            above, below = pl.ds(low + PAD - 1, BLOCK), pl.ds(low + PAD + 1, BLOCK)
            edge = lax.broadcasted_iota(jnp.int32, (BLOCK, GRID), 1)
            total = []
            for field in range(FIELDS):
                here = pad[field, mid, :]
                left = jnp.where(edge == 0, 0.0, pltpu.roll(here, 1, 1))
                right = jnp.where(edge == GRID - 1, 0.0, pltpu.roll(here, GRID - 1, 1))
                beside = pad[field, above, :] + pad[field, below, :] + left + right
                total.append(here - stiff[field // 2] * (4.0 * here - beside))
                if field < EDGE:
                    total[field] -= cross_own[field, at, :]
            for index, (later, stride) in enumerate(LOCAL):
                earlier = later - stride
                gaps = [pad[2 * later + c, mid, :] - pad[2 * earlier + c, mid, :] for c in range(2)]
                pulled = pull(len(CROSS) + index, at, pool[earlier, at, :].astype(F32), gaps[0], gaps[1], gain[earlier][stride - 1])
                for c in range(2):
                    total[2 * earlier + c] += pulled[c]
                    total[2 * later + c] -= pulled[c]
            for field in range(FIELDS):
                target[field, put, :] = total[field]

        over(seg, body)

    def finish(step, seg):
        target, base = goal(step)
        if seg < 2:
            side, row = ((1, 0), (0, GRID - 1))[seg]

            @pl.when((has_up, has_down)[seg])
            def _():
                rim_copy(step, side).wait_recv()

            for field in range(FIELDS):
                spot = slice(base + row, base + row + 1)
                target[field, spot, :] = target[field, spot, :] + stiff[field // 2] * rimrecv[step, side, field:field + 1, :]

        @pl.when(has_next)
        def _():
            f_back(step, seg).wait_recv()

        def body(low, at, mid):
            put = pl.ds(pl.multiple_of(low + base, PAD), BLOCK)
            for field in range(EDGE):
                done = target[EDGE + field, put, :] + frecv[step, field, at, :].astype(F32)
                target[EDGE + field, put, :] = done
                if step + 1 < ITERS:
                    usend[step + 1, field, at, :] = done.astype(BF16)

        over(seg, body)
        if step + 1 < ITERS:
            @pl.when(has_next)
            def _():
                u_forth(step + 1, seg).start()

            if seg == 1:
                keep_rims(step + 1, pads[step + 1])
                send_rims(step + 1)
        else:
            store(seg).start()

    def store(seg):
        at = rows_of(seg)
        return pltpu.make_async_copy(fin.at[:, at, :], out.at[:, at, :], loc_sem.at[5 + seg])


    @pl.when(has_prev)
    def _():
        for index in range(SKIPS):
            q_forth(index).wait_recv()


    for seg in segments:
        cross_turn(0, seg)


    def own_first(section, carry):
        own_pool(section)
        return carry

    lax.fori_loop(0, SKIPS, own_first, 0)


    def local_step(step, carry):
        late = (step >= 3).astype(jnp.int32)
        section = late * (3 + (step - 3) // 3) + (1 - late) * (1 + (step >= 1).astype(jnp.int32))
        stride = late * ((step - 3) % 3 + 1) + (1 - late) * (1 + (step >= 2).astype(jnp.int32))
        earlier = section - stride
        pair_cache(len(CROSS) + step, section, offsets[stride - 1, 0, earlier], offsets[stride - 1, 1, earlier])
        return carry

    lax.fori_loop(0, len(LOCAL), local_step, 0)

    for step in range(ITERS):
        for seg in segments:
            if step > 0:

                cross_turn(step, seg)

            local_pass(step, seg)
        for seg in segments:

            finish(step, seg)


    for seg in segments:
        store(seg).wait()

    @pl.when(has_prev)
    def _():
        for seg in segments:
            for step in range(ITERS):
                f_back(step, seg).wait_send()

    @pl.when(has_next)
    def _():
        facts_copy().wait_send()
        for index in range(SKIPS):
            q_forth(index).wait_send()
        for seg in segments:
            for step in range(ITERS):
                u_forth(step, seg).wait_send()

    for step in range(ITERS):
        @pl.when(has_up)
        def _():
            rim_copy(step, 0).wait_send()

        @pl.when(has_down)
        def _():
            rim_copy(step, 1).wait_send()


def local(images, displacement, offsets, weights, stiffness):
    anywhere = pl.BlockSpec(memory_space=pl.ANY)
    dma, vmem, smem = pltpu.SemaphoreType.DMA, pltpu.VMEM, pltpu.SMEM
    segs, cross = len(SEGS), len(CROSS)
    moved = pl.pallas_call(
        kernel,
        out_shape=jax.ShapeDtypeStruct((FIELDS, GRID, GRID), F32),
        in_specs=[anywhere] * 5,
        out_specs=anywhere,
        scratch_shapes=[
            vmem((RES, PIXELS, PIXELS), BF16),
            vmem((SKIPS + 1, 2 * REACH, HALF), BF16),
            vmem((SKIPS + 1, 2 * REACH, HALF), BF16),
            vmem((cross + len(LOCAL), 3, GRID, GRID), BF16),
            vmem((RES, GRID, GRID), BF16),
            vmem((SKIPS, GRID, GRID), BF16),
            vmem((FIELDS, GRID + 2 * PAD, GRID), F32),
            vmem((FIELDS, GRID + 2 * PAD, GRID), F32),
            vmem((FIELDS, GRID + 2 * PAD, GRID), F32),
            vmem((FIELDS, GRID, GRID), F32),
            vmem((EDGE, GRID, GRID), F32),
            vmem((ITERS, EDGE, GRID, GRID), BF16),
            vmem((ITERS, EDGE, GRID, GRID), BF16),
            vmem((ITERS, EDGE, GRID, GRID), BF16),
            vmem((ITERS, EDGE, GRID, GRID), BF16),
            vmem((ITERS, 2, 16, GRID), F32),
            vmem((ITERS, 2, 16, GRID), F32),
            vmem((8, 128), jnp.int32),
            vmem((8, 128), jnp.int32),
            smem((8, 128), jnp.int32),
            smem((SKIPS, 2, RES), jnp.int32),
            smem((SKIPS, RES), jnp.int32),
            smem((RES,), F32),
            dma((RES,)),
            dma((5 + segs,)),
            dma((ITERS, segs)),
            dma((ITERS, segs)),
            dma((ITERS, segs)),
            dma((ITERS, segs)),
            dma((SKIPS,)),
            dma((SKIPS,)),
            dma((ITERS, 2)),
            dma((ITERS, 2)),
            dma((2,)),
        ],
        compiler_params=pltpu.CompilerParams(collective_id=0, has_side_effects=True, vmem_limit_bytes=67_000_000),
    )(displacement.reshape(FIELDS, GRID, GRID), images, offsets.transpose(1, 2, 0), weights.T, stiffness)
    return moved.reshape(RES, 2, GRID, GRID)


def solution(mesh):
    placed = (
        P("sec", "tile", None),
        P("sec", None, "tile", None),
        P("sec", None, None),
        P("sec", None),
        P("sec"),
    )
    return jax.shard_map(
        local, mesh=mesh, in_specs=placed, out_specs=P("sec", None, "tile", None), check_vma=False
    )
```

time: 56.1 us -> 56.1 us (level)
  the two profiles are of different devices: /device:TPU:56 before, /device:TPU:22 now
where the time goes in v2:
time: 56.1 us; the launch traced here: 55.9 us
  Pallas kernels  53.8 us (96%)
  local copies, waits for them, and re-layouts  2.06 us (4%)
    pallas_call x1, Pallas kernels, local(): pl.pallas_call(kernel, out_shape=jax.ShapeDtypeStruct((FIELDS, GRID, GRID...  53.8 us
    unnamed x1, local copies, waits for them, and re-layouts  2.06 us

profile of v2, /device:TPU:22, one launch (start us, length us, event | category | flops | bytes accessed | tf_op | source)
XLA Modules:
  0.0 55.9 jit_solution(16432510565373669363)
XLA Ops:
  0.0 53.8 %shard_map.55 = f32[12,128,128]{2,1,0:T(8,128)} custom-call(f32[12,128,128]{2,1,0:T(8,128)} %bitcast.5, bf16[6,512,512]{2,1,0:T(8,128)(2,1)} %images.1, s32[3,2,6]{2,1,0:T(2,128)} %bitcast.6, s32[3,6]{1,0:T(4,128)} %bitcast.7, f32[6]{0:T(128)} %stiffness_hbm.1), custom_call_target="tpu_custom_call" | custom-call | tf_op jit(solution)/shard_map/pallas_call | solution.py:451
  53.8 2.1 %copy.7 = f32[6,2,128,128]{3,2,1,0:T(8,128)} copy(f32[6,2,128,128]{3,2,1,0:T(8,128)} %bitcast.4) | data formatting | bytes 1572864

commit v3 on v2

--- a/solution.py
+++ b/solution.py
@@ -19,16 +19,22 @@
 MEET = 2 * REACH - GRID
 F32, BF16 = jnp.float32, jnp.bfloat16
 MESH = pl.DeviceIdType.MESH
+X_SIZE, Z_LOW = 4, 8
 
 SEGS = ((0, 16), (112, 16), (16, 32), (48, 32), (80, 32))
-CROSS = ((0, 1), (0, 2), (0, 3), (1, 2), (1, 3), (2, 3))
-LOCAL = ((1, 1), (2, 1), (2, 2), (3, 1), (3, 2), (3, 3), (4, 1), (4, 2), (4, 3), (5, 1), (5, 2), (5, 3))
+PAIRS = tuple((later, stride) for later in range(RES) for stride in range(1, SKIPS + 1))
+CROSS = tuple(pair for pair in PAIRS if pair[0] < pair[1])
+LOCAL = tuple(pair for pair in PAIRS if pair[0] >= pair[1])
 
 kernel_sigma = 2.0
 force_step = 0.5
 elastic_step = 0.1
 
 
+def slot_of(later, stride):
+    return later * SKIPS + stride - 1
+
+
 def dot_rows(left, right):
     return lax.dot_general(left, right, (((1,), (1,)), ((), ())), preferred_element_type=F32)
 
@@ -39,8 +45,8 @@
 
 
 def kernel(disp, images, offsets_hbm, weights_hbm, stiffness_hbm, out, img, first_t, last_t, cache, pool, precv,
-           pad_a, pad_b, pad_c, fin, cross_own, usend, uprev, fsend, frecv, rimsend, rimrecv, meta_v, meta_r, meta_s,
-           offsets, weights, stiffness, img_sem, loc_sem, u_ssem, u_rsem, f_ssem, f_rsem, q_ssem, q_rsem, rim_ssem, rim_rsem, m_sem):
+           pad_a, pad_b, pad_c, fin, cross_own, usend, uprev, fsend, frecv, rimsend, rimrecv, meta_v, meta_r, meta_s, shift_s,
+           offsets, weights, stiffness, img_sem, loc_sem, u_ssem, u_rsem, f_ssem, f_rsem, q_ssem, q_rsem, rim_ssem, rim_rsem, m_sem, round_sem):
     me, col = lax.axis_index("sec"), lax.axis_index("tile")
     has_prev, has_next = me > 0, me < lax.axis_size("sec") - 1
     has_up, has_down = col > 0, col < lax.axis_size("tile") - 1
@@ -49,11 +55,32 @@
     segments = range(len(SEGS))
 
     barrier = pltpu.get_barrier_semaphore()
-    sides = ((has_prev, before), (has_next, after), (has_up, {"tile": col - 1}), (has_down, {"tile": col + 1}))
-    for there, target in sides:
+    rank = col % 4
+    height, across = (rank // 2) * Z_LOW + me // X_SIZE, me % X_SIZE
+
+    def along(shift):
+        to = height + shift
+        return (to >= 0) & (to < 2 * Z_LOW), {"sec": (to % Z_LOW) * X_SIZE + across, "tile": col - rank + (to // Z_LOW) * 2 + col % 2}
+
+    def count(*conditions):
+        return sum(condition.astype(jnp.int32) for condition in conditions)
+
+    def tell(semaphore, there, target):
         @pl.when(there)
         def _():
-            pl.semaphore_signal(barrier, inc=1, device_id=target, device_id_type=MESH)
+            pl.semaphore_signal(semaphore, inc=1, device_id=target, device_id_type=MESH)
+
+    last_col = lax.axis_size("tile") - 1
+    upper, lower = along(1), along(-1)
+    partner = {"tile": col + 1 - 2 * (col % 2)}
+    hears_y = ((rank == 3) & (col < last_col)) | ((rank == 0) & (col > 0))
+    tells_y = ((rank == 2) & (col > 2)) | ((rank == 1) & (col < last_col - 3))
+    hears_from = {"tile": jnp.where(rank == 3, col + 3, col - 3)}
+    tells_core = (rank == 0) | (rank == 3)
+    tells_to = {"tile": jnp.where(tells_core, col + 1 - 2 * (col % 2), jnp.where(rank == 1, col + 3, col - 3))}
+    has_far = (col > 0) & (col < last_col)
+    for there, target in ((has_prev, before), (has_next, after), upper, lower, (col >= 0, partner), (hears_y, hears_from)):
+        tell(barrier, there, target)
 
     scalars = [pltpu.make_async_copy(src, dst, loc_sem.at[place]) for place, (src, dst) in enumerate(
         ((offsets_hbm, offsets), (weights_hbm, weights), (stiffness_hbm, stiffness)))]
@@ -89,6 +116,7 @@
             ref[offset, REACH:2 * REACH, :] = (smooth * spread[half] / (kernel_sigma * kernel_sigma)).astype(BF16)
         return carry
 
+    lax.fori_loop(0, SKIPS + 1, table, 0)
     for copy in scalars:
         copy.wait()
 
@@ -101,6 +129,10 @@
             facts = jnp.where(lane == base + 1, offsets[stride, 1, section + SKIPS], facts)
             facts = jnp.where(lane == base + 2, weights[stride, section + SKIPS], facts)
     meta_v[...] = facts
+    for section in range(RES):
+        for stride in range(SKIPS):
+            for axis in range(2):
+                shift_s[axis, (section + SKIPS) * SKIPS + stride] = offsets[stride, axis, section]
     rimsend[...] = jnp.zeros_like(rimsend)
 
     @pl.when(jnp.logical_not(has_prev))
@@ -139,9 +171,9 @@
 
     keep_rims(0, pad_a)
 
-
-    pl.semaphore_wait(barrier, sum(there.astype(jnp.int32) for there, _ in sides))
-
+    pl.semaphore_wait(barrier, count(has_prev, has_next, upper[0], lower[0], col >= 0, tells_y))
+    tell(round_sem.at[0], *upper)
+    tell(round_sem.at[0], *lower)
 
     def remote(src, dst, send_sem, recv_sem, target):
         return pltpu.make_async_remote_copy(
@@ -181,13 +213,9 @@
     @pl.when(has_next)
     def _():
         facts_copy().start()
-        for seg in segments:
+        for seg in segments[:2]:
             u_forth(0, seg).start()
 
-    send_rims(0)
-
-
-    lax.fori_loop(0, SKIPS + 1, table, 0)
     zero_row = jnp.zeros((PAD, GRID), F32)
     for pad in pads:
         for field in range(FIELDS):
@@ -195,30 +223,34 @@
             pad[field, PAD + GRID:, :] = zero_row
 
     def columns(section, first, last, count):
-        parts = []
+        halves = []
         for low in (0, HALF):
             top = dot_rows(first, img[section, low:low + HALF, 0:HALF])
             bottom = dot_rows(last, img[section, low:low + HALF, HALF:])
-            parts.append(jnp.concatenate([
-                meet(top[REACH * one:REACH * (one + 1)], bottom[REACH * one:REACH * (one + 1)]) for one in range(count)], axis=0).astype(BF16))
-        return parts
-
-    def own_pool(section):
-        parts = columns(section, first_t[0, 0:REACH, :], last_t[0, 0:REACH, :], 1)
-        pool[section] = meet(dot_rows(first_t[0, 0:REACH, :], parts[0]), dot_rows(last_t[0, 0:REACH, :], parts[1])).astype(BF16)
-
-    def pair_cache(slot, section, off_r, off_c):
-        parts = columns(section, first_t[off_c], last_t[off_c], 2)
-        top, bottom = dot_rows(first_t[off_r], parts[0]), dot_rows(last_t[off_r], parts[1])
-        smooth = meet(top[:REACH], bottom[:REACH]).astype(BF16)
-        cache[slot, 0] = smooth[:, :GRID]
-        cache[slot, 1] = meet(top[REACH:, :GRID], bottom[REACH:, :GRID]).astype(BF16)
-        cache[slot, 2] = smooth[:, GRID:]
-
-
-    def own_step(section, carry):
+            halves.append([meet(top[REACH * one:REACH * (one + 1)], bottom[REACH * one:REACH * (one + 1)]).astype(BF16) for one in range(count)])
+        return halves
+
+    def section_pool(section):
+        shifts = []
+        for stride in range(1, SKIPS + 1):
+            place = (section - stride + SKIPS) * SKIPS + stride - 1
+            shifts.append((shift_s[0, place], shift_s[1, place]))
+        first = jnp.concatenate([first_t[off_c] for _, off_c in shifts] + [first_t[0, 0:REACH, :]], axis=0)
+        last = jnp.concatenate([last_t[off_c] for _, off_c in shifts] + [last_t[0, 0:REACH, :]], axis=0)
+        low, high = columns(section, first, last, 2 * SKIPS + 1)
+        for index, (off_r, _) in enumerate(shifts):
+            slot = section * SKIPS + index
+            top = dot_rows(first_t[off_r], jnp.concatenate(low[2 * index:2 * index + 2], axis=0))
+            bottom = dot_rows(last_t[off_r], jnp.concatenate(high[2 * index:2 * index + 2], axis=0))
+            smooth = meet(top[:REACH], bottom[:REACH]).astype(BF16)
+            cache[slot, 0] = smooth[:, :GRID]
+            cache[slot, 1] = meet(top[REACH:, :GRID], bottom[REACH:, :GRID]).astype(BF16)
+            cache[slot, 2] = smooth[:, GRID:]
+        pool[section] = meet(dot_rows(first_t[0, 0:REACH, :], low[-1]), dot_rows(last_t[0, 0:REACH, :], high[-1])).astype(BF16)
+
+    def late_step(section, carry):
         fetch(section).wait()
-        own_pool(section)
+        section_pool(section)
 
         @pl.when(has_next)
         def _():
@@ -226,11 +258,19 @@
 
         return carry
 
-    lax.fori_loop(SKIPS, RES, own_step, 0)
+    lax.fori_loop(SKIPS, RES - 1, late_step, 0)
+    pl.semaphore_wait(round_sem.at[0], count(upper[0], lower[0]))
+    tell(round_sem.at[1], *along(2))
+    tell(round_sem.at[1], *along(-2))
+    lax.fori_loop(RES - 1, RES, late_step, 0)
+
+    @pl.when(has_next)
+    def _():
+        for seg in segments[2:]:
+            u_forth(0, seg).start()
 
     for section in range(SKIPS):
         fetch(section).wait()
-
 
     @pl.when(has_prev)
     def _():
@@ -239,17 +279,22 @@
     to_scalars = pltpu.make_async_copy(meta_r, meta_s, loc_sem.at[4])
     to_scalars.start()
     to_scalars.wait()
-
-
-    def cross_step(slot, carry):
-        first, second = (slot >= 3).astype(jnp.int32), (slot >= 5).astype(jnp.int32)
-        section = first + second
-        stride = slot + 1 - 2 * first - second
-        base = ((section - stride + SKIPS) * SKIPS + stride - 1) * 3
-        pair_cache(slot, section, meta_s[0, base], meta_s[0, base + 1])
+    for place in range(SKIPS * SKIPS):
+        for axis in range(2):
+            shift_s[axis, place] = meta_s[0, 3 * place + axis]
+
+    pl.semaphore_wait(round_sem.at[1], count(along(2)[0], along(-2)[0]))
+    tell(round_sem.at[2], *along(4))
+    tell(round_sem.at[2], *along(-4))
+
+    def early_step(section, carry):
+        section_pool(section)
         return carry
 
-    lax.fori_loop(0, len(CROSS), cross_step, 0)
+    lax.fori_loop(0, SKIPS, early_step, 0)
+
+    pl.semaphore_wait(round_sem.at[2], count(along(4)[0], along(-4)[0]))
+    tell(round_sem.at[3], tells_core | tells_y, tells_to)
 
     gain = [[force_step * weights[k - 1, s].astype(F32) for k in range(1, SKIPS + 1)] for s in range(RES)]
     stiff = [elastic_step * stiffness[s] for s in range(RES)]
@@ -279,10 +324,10 @@
 
         def body(low, at, mid):
             own, back = [None] * EDGE, [None] * EDGE
-            for slot, (later, stride) in enumerate(CROSS):
+            for index, (later, stride) in enumerate(CROSS):
                 earlier = later - stride + SKIPS
                 gaps = [pad[2 * later + c, mid, :] - uprev[step, 2 * earlier + c, at, :].astype(F32) for c in range(2)]
-                pulled = pull(slot, at, precv[earlier, at, :].astype(F32), gaps[0], gaps[1], cross_gain[slot])
+                pulled = pull(slot_of(later, stride), at, precv[earlier, at, :].astype(F32), gaps[0], gaps[1], cross_gain[index])
                 for c in range(2):
                     here, there = 2 * later + c, 2 * earlier + c
                     own[here] = pulled[c] if own[here] is None else own[here] + pulled[c]
@@ -323,10 +368,10 @@
                 total.append(here - stiff[field // 2] * (4.0 * here - beside))
                 if field < EDGE:
                     total[field] -= cross_own[field, at, :]
-            for index, (later, stride) in enumerate(LOCAL):
+            for later, stride in LOCAL:
                 earlier = later - stride
                 gaps = [pad[2 * later + c, mid, :] - pad[2 * earlier + c, mid, :] for c in range(2)]
-                pulled = pull(len(CROSS) + index, at, pool[earlier, at, :].astype(F32), gaps[0], gaps[1], gain[earlier][stride - 1])
+                pulled = pull(slot_of(later, stride), at, pool[earlier, at, :].astype(F32), gaps[0], gaps[1], gain[earlier][stride - 1])
                 for c in range(2):
                     total[2 * earlier + c] += pulled[c]
                     total[2 * later + c] -= pulled[c]
@@ -376,45 +421,27 @@
         at = rows_of(seg)
         return pltpu.make_async_copy(fin.at[:, at, :], out.at[:, at, :], loc_sem.at[5 + seg])
 
-
     @pl.when(has_prev)
     def _():
         for index in range(SKIPS):
             q_forth(index).wait_recv()
 
-
     for seg in segments:
         cross_turn(0, seg)
 
-
-    def own_first(section, carry):
-        own_pool(section)
-        return carry
-
-    lax.fori_loop(0, SKIPS, own_first, 0)
-
-
-    def local_step(step, carry):
-        late = (step >= 3).astype(jnp.int32)
-        section = late * (3 + (step - 3) // 3) + (1 - late) * (1 + (step >= 1).astype(jnp.int32))
-        stride = late * ((step - 3) % 3 + 1) + (1 - late) * (1 + (step >= 2).astype(jnp.int32))
-        earlier = section - stride
-        pair_cache(len(CROSS) + step, section, offsets[stride - 1, 0, earlier], offsets[stride - 1, 1, earlier])
-        return carry
-
-    lax.fori_loop(0, len(LOCAL), local_step, 0)
+    @pl.when(has_far)
+    def _():
+        pl.semaphore_wait(round_sem.at[3], 1)
+
+    send_rims(0)
 
     for step in range(ITERS):
         for seg in segments:
             if step > 0:
-
                 cross_turn(step, seg)
-
             local_pass(step, seg)
         for seg in segments:
-
             finish(step, seg)
-
 
     for seg in segments:
         store(seg).wait()
@@ -447,7 +474,7 @@
 def local(images, displacement, offsets, weights, stiffness):
     anywhere = pl.BlockSpec(memory_space=pl.ANY)
     dma, vmem, smem = pltpu.SemaphoreType.DMA, pltpu.VMEM, pltpu.SMEM
-    segs, cross = len(SEGS), len(CROSS)
+    segs = len(SEGS)
     moved = pl.pallas_call(
         kernel,
         out_shape=jax.ShapeDtypeStruct((FIELDS, GRID, GRID), F32),
@@ -457,7 +484,7 @@
             vmem((RES, PIXELS, PIXELS), BF16),
             vmem((SKIPS + 1, 2 * REACH, HALF), BF16),
             vmem((SKIPS + 1, 2 * REACH, HALF), BF16),
-            vmem((cross + len(LOCAL), 3, GRID, GRID), BF16),
+            vmem((len(PAIRS), 3, GRID, GRID), BF16),
             vmem((RES, GRID, GRID), BF16),
             vmem((SKIPS, GRID, GRID), BF16),
             vmem((FIELDS, GRID + 2 * PAD, GRID), F32),
@@ -474,6 +501,7 @@
             vmem((8, 128), jnp.int32),
             vmem((8, 128), jnp.int32),
             smem((8, 128), jnp.int32),
+            smem((2, (RES + SKIPS) * SKIPS), jnp.int32),
             smem((SKIPS, 2, RES), jnp.int32),
             smem((SKIPS, RES), jnp.int32),
             smem((RES,), F32),
@@ -488,6 +516,7 @@
             dma((ITERS, 2)),
             dma((ITERS, 2)),
             dma((2,)),
+            pltpu.SemaphoreType.REGULAR((4,)),
         ],
         compiler_params=pltpu.CompilerParams(collective_id=0, has_side_effects=True, vmem_limit_bytes=67_000_000),
     )(displacement.reshape(FIELDS, GRID, GRID), images, offsets.transpose(1, 2, 0), weights.T, stiffness)

time: 56.1 us -> 50.8 us (0.906)
  Pallas kernels: 53.8 us -> 48.5 us
    pallas_call x1, Pallas kernels: 53.8 us -> 48.5 us  [local(): pl.pallas_call(kernel, out_shape=jax.ShapeDtypeStruct((FIELDS, GRID, GRID...]
where the time goes in v3:
time: 50.8 us; the launch traced here: 50.6 us
  Pallas kernels  48.5 us (95%)
  local copies, waits for them, and re-layouts  2.06 us (4%)
    pallas_call x1, Pallas kernels, local(): pl.pallas_call(kernel, out_shape=jax.ShapeDtypeStruct((FIELDS, GRID, GRID...  48.5 us
    unnamed x1, local copies, waits for them, and re-layouts  2.06 us

profile of v3, /device:TPU:22, one launch (start us, length us, event | category | flops | bytes accessed | tf_op | source)
XLA Modules:
  0.0 50.6 jit_solution(11052475197614916862)
XLA Ops:
  0.0 48.5 %shard_map.55 = f32[12,128,128]{2,1,0:T(8,128)} custom-call(f32[12,128,128]{2,1,0:T(8,128)} %bitcast.5, bf16[6,512,512]{2,1,0:T(8,128)(2,1)} %images.1, s32[3,2,6]{2,1,0:T(2,128)} %bitcast.6, s32[3,6]{1,0:T(4,128)} %bitcast.7, f32[6]{0:T(128)} %stiffness_hbm.1), custom_call_target="tpu_custom_call" | custom-call | tf_op jit(solution)/shard_map/pallas_call | solution.py:478
  48.5 2.1 %copy.7 = f32[6,2,128,128]{3,2,1,0:T(8,128)} copy(f32[6,2,128,128]{3,2,1,0:T(8,128)} %bitcast.4) | data formatting | bytes 1572864

commit v4 on v3

--- a/solution.py
+++ b/solution.py
@@ -22,6 +22,7 @@
 X_SIZE, Z_LOW = 4, 8
 
 SEGS = ((0, 16), (112, 16), (16, 32), (48, 32), (80, 32))
+ORDER = (2, 3, 4, 0, 1)
 PAIRS = tuple((later, stride) for later in range(RES) for stride in range(1, SKIPS + 1))
 CROSS = tuple(pair for pair in PAIRS if pair[0] < pair[1])
 LOCAL = tuple(pair for pair in PAIRS if pair[0] >= pair[1])
@@ -117,6 +118,29 @@
         return carry
 
     lax.fori_loop(0, SKIPS + 1, table, 0)
+    pl.semaphore_wait(barrier, count(has_prev, has_next, upper[0], lower[0], col >= 0, tells_y))
+
+    def within(low, high):
+        return (height >= low) & (height <= high)
+
+    def hear(place, there):
+        @pl.when(there)
+        def _():
+            pl.semaphore_wait(round_sem.at[place], 1)
+
+    def pass_up(low, high):
+        here = within(low, high)
+        hear(0, here & lower[0])
+        there, target = upper
+        tell(round_sem.at[0], here & there, target)
+        tell(round_sem.at[4], here & (height >= Z_LOW) & (tells_core | tells_y), tells_to)
+
+    def pass_down(step, low, high):
+        _, target = along(-(1 << step))
+        tell(round_sem.at[1 + step], within(low, high), target)
+
+    pass_down(0, 7, 14)
+    pass_up(0, 9)
     for copy in scalars:
         copy.wait()
 
@@ -170,10 +194,6 @@
             rimsend[step, 1, field:field + 1, :] = source[field, PAD + GRID - 1:PAD + GRID, :]
 
     keep_rims(0, pad_a)
-
-    pl.semaphore_wait(barrier, count(has_prev, has_next, upper[0], lower[0], col >= 0, tells_y))
-    tell(round_sem.at[0], *upper)
-    tell(round_sem.at[0], *lower)
 
     def remote(src, dst, send_sem, recv_sem, target):
         return pltpu.make_async_remote_copy(
@@ -258,11 +278,13 @@
 
         return carry
 
+    pass_up(10, 11)
     lax.fori_loop(SKIPS, RES - 1, late_step, 0)
-    pl.semaphore_wait(round_sem.at[0], count(upper[0], lower[0]))
-    tell(round_sem.at[1], *along(2))
-    tell(round_sem.at[1], *along(-2))
+    pass_up(12, 13)
     lax.fori_loop(RES - 1, RES, late_step, 0)
+    pass_up(14, 15)
+    hear(1, within(6, 13))
+    pass_down(1, 6, 13)
 
     @pl.when(has_next)
     def _():
@@ -283,18 +305,28 @@
         for axis in range(2):
             shift_s[axis, place] = meta_s[0, 3 * place + axis]
 
-    pl.semaphore_wait(round_sem.at[1], count(along(2)[0], along(-2)[0]))
-    tell(round_sem.at[2], *along(4))
-    tell(round_sem.at[2], *along(-4))
-
+    def open_rims(low, high):
+        here = within(low, high)
+        hear(4, here & has_far)
+
+        @pl.when(here & has_up)
+        def _():
+            rim_copy(0, 0).start()
+
+        @pl.when(here & has_down)
+        def _():
+            rim_copy(0, 1).start()
+
+    open_rims(8, 11)
     def early_step(section, carry):
         section_pool(section)
         return carry
 
     lax.fori_loop(0, SKIPS, early_step, 0)
 
-    pl.semaphore_wait(round_sem.at[2], count(along(4)[0], along(-4)[0]))
-    tell(round_sem.at[3], tells_core | tells_y, tells_to)
+    open_rims(12, 15)
+    hear(2, within(4, 11))
+    pass_down(2, 4, 11)
 
     gain = [[force_step * weights[k - 1, s].astype(F32) for k in range(1, SKIPS + 1)] for s in range(RES)]
     stiff = [elastic_step * stiffness[s] for s in range(RES)]
@@ -426,21 +458,22 @@
         for index in range(SKIPS):
             q_forth(index).wait_recv()
 
-    for seg in segments:
+    for seg in ORDER:
         cross_turn(0, seg)
-
-    @pl.when(has_far)
-    def _():
-        pl.semaphore_wait(round_sem.at[3], 1)
-
-    send_rims(0)
+    for seg in ORDER:
+        local_pass(0, seg)
+    hear(3, within(0, 7))
+    tell(round_sem.at[4], within(0, 7) & (tells_core | tells_y), tells_to)
+    open_rims(0, 7)
 
     for step in range(ITERS):
-        for seg in segments:
-            if step > 0:
-                cross_turn(step, seg)
-            local_pass(step, seg)
-        for seg in segments:
+        if step > 0:
+            for group in (ORDER[:3], ORDER[3:]):
+                for seg in group:
+                    cross_turn(step, seg)
+                for seg in group:
+                    local_pass(step, seg)
+        for seg in ORDER:
             finish(step, seg)
 
     for seg in segments:
@@ -516,7 +549,7 @@
             dma((ITERS, 2)),
             dma((ITERS, 2)),
             dma((2,)),
-            pltpu.SemaphoreType.REGULAR((4,)),
+            pltpu.SemaphoreType.REGULAR((5,)),
         ],
         compiler_params=pltpu.CompilerParams(collective_id=0, has_side_effects=True, vmem_limit_bytes=67_000_000),
     )(displacement.reshape(FIELDS, GRID, GRID), images, offsets.transpose(1, 2, 0), weights.T, stiffness)

time: 50.8 us -> 49.2 us (0.969)
  the two profiles are of different devices: /device:TPU:22 before, /device:TPU:111 now
where the time goes in v4:
time: 49.2 us; the launch traced here: 49.1 us
  Pallas kernels  47 us (96%)
  local copies, waits for them, and re-layouts  2.06 us (4%)
    pallas_call x1, Pallas kernels, local(): pl.pallas_call(kernel, out_shape=jax.ShapeDtypeStruct((FIELDS, GRID, GRID...  47 us
    unnamed x1, local copies, waits for them, and re-layouts  2.06 us

profile of v4, /device:TPU:111, one launch (start us, length us, event | category | flops | bytes accessed | tf_op | source)
XLA Modules:
  0.0 49.1 jit_solution(18367544561477924906)
XLA Ops:
  0.0 47.0 %shard_map.55 = f32[12,128,128]{2,1,0:T(8,128)} custom-call(f32[12,128,128]{2,1,0:T(8,128)} %bitcast.5, bf16[6,512,512]{2,1,0:T(8,128)(2,1)} %images.1, s32[3,2,6]{2,1,0:T(2,128)} %bitcast.6, s32[3,6]{1,0:T(4,128)} %bitcast.7, f32[6]{0:T(128)} %stiffness_hbm.1), custom_call_target="tpu_custom_call" | custom-call | tf_op jit(solution)/shard_map/pallas_call | solution.py:511
  47.0 2.1 %copy.7 = f32[6,2,128,128]{3,2,1,0:T(8,128)} copy(f32[6,2,128,128]{3,2,1,0:T(8,128)} %bitcast.4) | data formatting | bytes 1572864

commit v5 on v3

--- a/solution.py
+++ b/solution.py
@@ -19,7 +19,6 @@
 MEET = 2 * REACH - GRID
 F32, BF16 = jnp.float32, jnp.bfloat16
 MESH = pl.DeviceIdType.MESH
-X_SIZE, Z_LOW = 4, 8
 
 SEGS = ((0, 16), (112, 16), (16, 32), (48, 32), (80, 32))
 PAIRS = tuple((later, stride) for later in range(RES) for stride in range(1, SKIPS + 1))
@@ -55,31 +54,17 @@
     segments = range(len(SEGS))
 
     barrier = pltpu.get_barrier_semaphore()
-    rank = col % 4
-    height, across = (rank // 2) * Z_LOW + me // X_SIZE, me % X_SIZE
-
-    def along(shift):
-        to = height + shift
-        return (to >= 0) & (to < 2 * Z_LOW), {"sec": (to % Z_LOW) * X_SIZE + across, "tile": col - rank + (to // Z_LOW) * 2 + col % 2}
-
-    def count(*conditions):
-        return sum(condition.astype(jnp.int32) for condition in conditions)
+    low_half, high_half = col % 4 < 2, col % 4 >= 2
+    odd = col % 2
+    partner, far = {"tile": col + 1 - 2 * odd}, {"tile": col - 1 + 2 * odd}
+    has_far = (col > 0) & (col < lax.axis_size("tile") - 1)
 
     def tell(semaphore, there, target):
         @pl.when(there)
         def _():
             pl.semaphore_signal(semaphore, inc=1, device_id=target, device_id_type=MESH)
 
-    last_col = lax.axis_size("tile") - 1
-    upper, lower = along(1), along(-1)
-    partner = {"tile": col + 1 - 2 * (col % 2)}
-    hears_y = ((rank == 3) & (col < last_col)) | ((rank == 0) & (col > 0))
-    tells_y = ((rank == 2) & (col > 2)) | ((rank == 1) & (col < last_col - 3))
-    hears_from = {"tile": jnp.where(rank == 3, col + 3, col - 3)}
-    tells_core = (rank == 0) | (rank == 3)
-    tells_to = {"tile": jnp.where(tells_core, col + 1 - 2 * (col % 2), jnp.where(rank == 1, col + 3, col - 3))}
-    has_far = (col > 0) & (col < last_col)
-    for there, target in ((has_prev, before), (has_next, after), upper, lower, (col >= 0, partner), (hears_y, hears_from)):
+    for there, target in ((low_half & has_far, far), (has_prev, before), (has_next, after), (col >= 0, partner)):
         tell(barrier, there, target)
 
     scalars = [pltpu.make_async_copy(src, dst, loc_sem.at[place]) for place, (src, dst) in enumerate(
@@ -116,6 +101,8 @@
             ref[offset, REACH:2 * REACH, :] = (smooth * spread[half] / (kernel_sigma * kernel_sigma)).astype(BF16)
         return carry
 
+    pl.semaphore_wait(barrier, sum(there.astype(jnp.int32) for there in (has_prev, has_next, col >= 0, high_half & has_far)))
+    tell(round_sem, high_half & has_far, far)
     lax.fori_loop(0, SKIPS + 1, table, 0)
     for copy in scalars:
         copy.wait()
@@ -171,10 +158,6 @@
 
     keep_rims(0, pad_a)
 
-    pl.semaphore_wait(barrier, count(has_prev, has_next, upper[0], lower[0], col >= 0, tells_y))
-    tell(round_sem.at[0], *upper)
-    tell(round_sem.at[0], *lower)
-
     def remote(src, dst, send_sem, recv_sem, target):
         return pltpu.make_async_remote_copy(
             src_ref=src, dst_ref=dst, send_sem=send_sem, recv_sem=recv_sem, device_id=target, device_id_type=MESH)
@@ -215,6 +198,10 @@
         facts_copy().start()
         for seg in segments[:2]:
             u_forth(0, seg).start()
+
+    @pl.when(high_half)
+    def _():
+        send_rims(0)
 
     zero_row = jnp.zeros((PAD, GRID), F32)
     for pad in pads:
@@ -258,11 +245,7 @@
 
         return carry
 
-    lax.fori_loop(SKIPS, RES - 1, late_step, 0)
-    pl.semaphore_wait(round_sem.at[0], count(upper[0], lower[0]))
-    tell(round_sem.at[1], *along(2))
-    tell(round_sem.at[1], *along(-2))
-    lax.fori_loop(RES - 1, RES, late_step, 0)
+    lax.fori_loop(SKIPS, RES, late_step, 0)
 
     @pl.when(has_next)
     def _():
@@ -283,18 +266,11 @@
         for axis in range(2):
             shift_s[axis, place] = meta_s[0, 3 * place + axis]
 
-    pl.semaphore_wait(round_sem.at[1], count(along(2)[0], along(-2)[0]))
-    tell(round_sem.at[2], *along(4))
-    tell(round_sem.at[2], *along(-4))
-
     def early_step(section, carry):
         section_pool(section)
         return carry
 
     lax.fori_loop(0, SKIPS, early_step, 0)
-
-    pl.semaphore_wait(round_sem.at[2], count(along(4)[0], along(-4)[0]))
-    tell(round_sem.at[3], tells_core | tells_y, tells_to)
 
     gain = [[force_step * weights[k - 1, s].astype(F32) for k in range(1, SKIPS + 1)] for s in range(RES)]
     stiff = [elastic_step * stiffness[s] for s in range(RES)]
@@ -428,20 +404,47 @@
 
     for seg in segments:
         cross_turn(0, seg)
-
-    @pl.when(has_far)
-    def _():
-        pl.semaphore_wait(round_sem.at[3], 1)
-
-    send_rims(0)
-
-    for step in range(ITERS):
-        for seg in segments:
-            if step > 0:
-                cross_turn(step, seg)
+    for seg in segments:
+        local_pass(0, seg)
+    edges, inner = segments[:2], segments[2:]
+
+    def turns(step, group):
+        for seg in group:
+            cross_turn(step, seg)
+
+    def passes(step, group):
+        for seg in group:
             local_pass(step, seg)
-        for seg in segments:
+
+    def finishes(step, group):
+        for seg in group:
             finish(step, seg)
+
+    @pl.when(high_half)
+    def _():
+        finishes(0, segments)
+        for step in range(1, ITERS):
+            turns(step, edges)
+            passes(step, edges)
+            turns(step, inner)
+            passes(step, inner)
+            finishes(step, segments)
+
+    @pl.when(low_half)
+    def _():
+        finishes(0, inner)
+        @pl.when(has_far)
+        def _():
+            pl.semaphore_wait(round_sem, 1)
+
+        send_rims(0)
+        for step in range(1, ITERS):
+            turns(step, inner)
+            finishes(step - 1, edges)
+            turns(step, edges)
+            passes(step, segments)
+            finishes(step, inner)
+        finishes(ITERS - 1, edges)
 
     for seg in segments:
         store(seg).wait()
@@ -516,7 +519,7 @@
             dma((ITERS, 2)),
             dma((ITERS, 2)),
             dma((2,)),
-            pltpu.SemaphoreType.REGULAR((4,)),
+            pltpu.SemaphoreType.REGULAR,
         ],
         compiler_params=pltpu.CompilerParams(collective_id=0, has_side_effects=True, vmem_limit_bytes=67_000_000),
     )(displacement.reshape(FIELDS, GRID, GRID), images, offsets.transpose(1, 2, 0), weights.T, stiffness)

time: 50.8 us -> 47 us (0.925)
  the two profiles are of different devices: /device:TPU:22 before, /device:TPU:463 now
where the time goes in v5:
time: 47 us; the launch traced here: 46.9 us
  Pallas kernels  44.9 us (96%)
  local copies, waits for them, and re-layouts  2.06 us (4%)
    pallas_call x1, Pallas kernels, local(): pl.pallas_call(kernel, out_shape=jax.ShapeDtypeStruct((FIELDS, GRID, GRID...  44.9 us
    unnamed x1, local copies, waits for them, and re-layouts  2.06 us

profile of v5, /device:TPU:463, one launch (start us, length us, event | category | flops | bytes accessed | tf_op | source)
XLA Modules:
  0.0 46.9 jit_solution(728987794129260290)
XLA Ops:
  0.0 44.9 %shard_map.55 = f32[12,128,128]{2,1,0:T(8,128)} custom-call(f32[12,128,128]{2,1,0:T(8,128)} %bitcast.5, bf16[6,512,512]{2,1,0:T(8,128)(2,1)} %images.1, s32[3,2,6]{2,1,0:T(2,128)} %bitcast.6, s32[3,6]{1,0:T(4,128)} %bitcast.7, f32[6]{0:T(128)} %stiffness_hbm.1), custom_call_target="tpu_custom_call" | custom-call | tf_op jit(solution)/shard_map/pallas_call | solution.py:481
  44.9 2.1 %copy.7 = f32[6,2,128,128]{3,2,1,0:T(8,128)} copy(f32[6,2,128,128]{3,2,1,0:T(8,128)} %bitcast.4) | data formatting | bytes 1572864

commit v6 on v5

--- a/solution.py
+++ b/solution.py
@@ -101,8 +101,6 @@
             ref[offset, REACH:2 * REACH, :] = (smooth * spread[half] / (kernel_sigma * kernel_sigma)).astype(BF16)
         return carry
 
-    pl.semaphore_wait(barrier, sum(there.astype(jnp.int32) for there in (has_prev, has_next, col >= 0, high_half & has_far)))
-    tell(round_sem, high_half & has_far, far)
     lax.fori_loop(0, SKIPS + 1, table, 0)
     for copy in scalars:
         copy.wait()
@@ -158,6 +156,9 @@
 
     keep_rims(0, pad_a)
 
+    pl.semaphore_wait(barrier, sum(there.astype(jnp.int32) for there in (has_prev, has_next, col >= 0, high_half & has_far)))
+    tell(round_sem, high_half & has_far, far)
+
     def remote(src, dst, send_sem, recv_sem, target):
         return pltpu.make_async_remote_copy(
             src_ref=src, dst_ref=dst, send_sem=send_sem, recv_sem=recv_sem, device_id=target, device_id_type=MESH)
@@ -177,8 +178,9 @@
         at = rows_of(seg)
         return remote(fsend.at[step, :, at, :], frecv.at[step, :, at, :], f_ssem.at[step, seg], f_rsem.at[step, seg], before)
 
-    def q_forth(index):
-        return remote(pool.at[index + SKIPS], precv.at[index], q_ssem.at[index], q_rsem.at[index], after)
+    def q_forth(seg):
+        at = rows_of(seg)
+        return remote(pool.at[pl.ds(SKIPS, SKIPS), at, :], precv.at[:, at, :], q_ssem.at[seg], q_rsem.at[seg], after)
 
     def rim_copy(step, side):
         target = {"tile": col - 1 if side == 0 else col + 1}
@@ -196,7 +198,7 @@
     @pl.when(has_next)
     def _():
         facts_copy().start()
-        for seg in segments[:2]:
+        for seg in segments:
             u_forth(0, seg).start()
 
     @pl.when(high_half)
@@ -238,19 +240,14 @@
     def late_step(section, carry):
         fetch(section).wait()
         section_pool(section)
-
-        @pl.when(has_next)
-        def _():
-            q_forth(section - SKIPS).start()
-
         return carry
 
     lax.fori_loop(SKIPS, RES, late_step, 0)
 
     @pl.when(has_next)
     def _():
-        for seg in segments[2:]:
-            u_forth(0, seg).start()
+        for seg in segments:
+            q_forth(seg).start()
 
     for section in range(SKIPS):
         fetch(section).wait()
@@ -318,6 +315,8 @@
         @pl.when(has_prev)
         def _():
             u_forth(step, seg).wait_recv()
+            if step == 0:
+                q_forth(seg).wait_recv()
 
         cross_pass(step, seg)
 
@@ -397,54 +396,62 @@
         at = rows_of(seg)
         return pltpu.make_async_copy(fin.at[:, at, :], out.at[:, at, :], loc_sem.at[5 + seg])
 
-    @pl.when(has_prev)
-    def _():
-        for index in range(SKIPS):
-            q_forth(index).wait_recv()
-
-    for seg in segments:
-        cross_turn(0, seg)
-    for seg in segments:
-        local_pass(0, seg)
     edges, inner = segments[:2], segments[2:]
 
-    def turns(step, group):
+    def turns(step, *group):
         for seg in group:
             cross_turn(step, seg)
 
-    def passes(step, group):
+    def passes(step, *group):
         for seg in group:
             local_pass(step, seg)
 
-    def finishes(step, group):
+    def finishes(step, *group):
         for seg in group:
             finish(step, seg)
 
+    for seg in segments:
+        turns(0, seg)
+        passes(0, seg)
+
     @pl.when(high_half)
     def _():
-        finishes(0, segments)
-        for step in range(1, ITERS):
-            turns(step, edges)
-            passes(step, edges)
-            turns(step, inner)
-            passes(step, inner)
-            finishes(step, segments)
+        finishes(0, 2, 0, 1, 3, 4)
+        turns(1, 2, 0, 1)
+        passes(1, 0, 1, 2)
+        turns(1, 3)
+        passes(1, 3)
+        finishes(1, 0, 1)
+        turns(1, 4)
+        passes(1, 4)
+        finishes(1, 2)
+        turns(2, 0, 1)
+        finishes(1, 3, 4)
+        passes(2, 0, 1)
+        turns(2, 2)
+        passes(2, 2)
+        turns(2, 3)
+        passes(2, 3)
+        turns(2, 4)
+        passes(2, 4)
+        finishes(2, 2, 3, 4, 0, 1)
 
     @pl.when(low_half)
     def _():
-        finishes(0, inner)
+        finishes(0, *inner)
         @pl.when(has_far)
         def _():
             pl.semaphore_wait(round_sem, 1)
 
         send_rims(0)
         for step in range(1, ITERS):
-            turns(step, inner)
-            finishes(step - 1, edges)
-            turns(step, edges)
-            passes(step, segments)
-            finishes(step, inner)
-        finishes(ITERS - 1, edges)
+            turns(step, *inner)
+            finishes(step - 1, *edges)
+            passes(step, *inner)
+            turns(step, *edges)
+            passes(step, *edges)
+            finishes(step, *inner)
+        finishes(ITERS - 1, *edges)
 
     for seg in segments:
         store(seg).wait()
@@ -458,8 +465,8 @@
     @pl.when(has_next)
     def _():
         facts_copy().wait_send()
-        for index in range(SKIPS):
-            q_forth(index).wait_send()
+        for seg in segments:
+            q_forth(seg).wait_send()
         for seg in segments:
             for step in range(ITERS):
                 u_forth(step, seg).wait_send()
@@ -478,6 +485,7 @@
     anywhere = pl.BlockSpec(memory_space=pl.ANY)
     dma, vmem, smem = pltpu.SemaphoreType.DMA, pltpu.VMEM, pltpu.SMEM
     segs = len(SEGS)
+    given = (displacement.reshape(FIELDS, GRID, GRID), images, offsets.transpose(1, 2, 0), weights.T, stiffness)
     moved = pl.pallas_call(
         kernel,
         out_shape=jax.ShapeDtypeStruct((FIELDS, GRID, GRID), F32),
@@ -514,15 +522,15 @@
             dma((ITERS, segs)),
             dma((ITERS, segs)),
             dma((ITERS, segs)),
-            dma((SKIPS,)),
-            dma((SKIPS,)),
+            dma((segs,)),
+            dma((segs,)),
             dma((ITERS, 2)),
             dma((ITERS, 2)),
             dma((2,)),
             pltpu.SemaphoreType.REGULAR,
         ],
-        compiler_params=pltpu.CompilerParams(collective_id=0, has_side_effects=True, vmem_limit_bytes=67_000_000),
-    )(displacement.reshape(FIELDS, GRID, GRID), images, offsets.transpose(1, 2, 0), weights.T, stiffness)
+        compiler_params=pltpu.CompilerParams(collective_id=0, has_side_effects=True, vmem_limit_bytes=24 << 20),
+    )(*(pltpu.with_memory_space_constraint(each, pltpu.HBM) for each in given))
     return moved.reshape(RES, 2, GRID, GRID)
 
 

time: 47 us -> 44.4 us (0.945)
  the two profiles are of different devices: /device:TPU:463 before, /device:TPU:393 now
where the time goes in v6:
time: 44.4 us; the launch traced here: 44.3 us
  Pallas kernels  43.4 us (98%)
  local copies, waits for them, and re-layouts  0.88 us (2%)
    pallas_call x1, Pallas kernels, local(): pl.pallas_call(kernel, out_shape=jax.ShapeDtypeStruct((FIELDS, GRID, GRID...  43.4 us

profile of v6, /device:TPU:393, one launch (start us, length us, event | category | flops | bytes accessed | tf_op | source)
XLA Modules:
  0.0 44.3 jit_solution(147822323300158416)
XLA Ops:
  0.0 43.4 %shard_map.55 = f32[12,128,128]{2,1,0:T(8,128)S(1)} custom-call(f32[12,128,128]{2,1,0:T(8,128)} %bitcast.5, bf16[6,512,512]{2,1,0:T(8,128)(2,1)} %images.1, s32[3,2,6]{2,1,0:T(2,128)} %bitcast.6, s32[3,6]{1,0:T(4,128)} %bitcast.7, f32[6]{0:T(128)} %stiffness_hbm.1), custom_call_target="tpu_custom_call" | custom-call | tf_op jit(solution)/shard_map/pallas_call | solution.py:489
  43.4 0.9 %copy.7 = f32[6,2,128,128]{3,2,1,0:T(8,128)} copy(f32[6,2,128,128]{3,2,1,0:T(8,128)S(1)} %bitcast.4) | data formatting | bytes 1572864

commit v7 on v6

--- a/solution.py
+++ b/solution.py
@@ -198,7 +198,7 @@
     @pl.when(has_next)
     def _():
         facts_copy().start()
-        for seg in segments:
+        for seg in segments[:3]:
             u_forth(0, seg).start()
 
     @pl.when(high_half)
@@ -247,6 +247,8 @@
     @pl.when(has_next)
     def _():
         for seg in segments:
+            if seg >= 3:
+                u_forth(0, seg).start()
             q_forth(seg).start()
 
     for section in range(SKIPS):
@@ -410,15 +412,32 @@
         for seg in group:
             finish(step, seg)
 
-    for seg in segments:
-        turns(0, seg)
-        passes(0, seg)
-
-    @pl.when(high_half)
-    def _():
-        finishes(0, 2, 0, 1, 3, 4)
-        turns(1, 2, 0, 1)
-        passes(1, 0, 1, 2)
+    turns(0, 0, 1, 2)
+    passes(0, 0, 1)
+    turns(0, 3)
+    passes(0, 2)
+    turns(0, 4)
+    passes(0, 3, 4)
+
+    @pl.when(low_half)
+    def _():
+        @pl.when(has_far)
+        def _():
+            pl.semaphore_wait(round_sem, 1)
+
+        send_rims(0)
+
+    early = low_half & (me < lax.axis_size("sec") // 2)
+
+    @pl.when(jnp.logical_not(early))
+    def _():
+        finishes(0, *edges)
+        finishes(0, 2)
+        turns(1, *edges)
+        finishes(0, 3, 4)
+        passes(1, 0, 1)
+        turns(1, 2)
+        passes(1, 2)
         turns(1, 3)
         passes(1, 3)
         finishes(1, 0, 1)
@@ -436,14 +455,9 @@
         passes(2, 4)
         finishes(2, 2, 3, 4, 0, 1)
 
-    @pl.when(low_half)
+    @pl.when(early)
     def _():
         finishes(0, *inner)
-        @pl.when(has_far)
-        def _():
-            pl.semaphore_wait(round_sem, 1)
-
-        send_rims(0)
         for step in range(1, ITERS):
             turns(step, *inner)
             finishes(step - 1, *edges)

time: 44.4 us -> 47.5 us (1.070)
  the two profiles are of different devices: /device:TPU:393 before, /device:TPU:103 now
where the time goes in v7:
time: 47.5 us; the launch traced here: 47.3 us
  Pallas kernels  46.5 us (98%)
  local copies, waits for them, and re-layouts  0.88 us (2%)
    pallas_call x1, Pallas kernels, local(): pl.pallas_call(kernel, out_shape=jax.ShapeDtypeStruct((FIELDS, GRID, GRID...  46.5 us

profile of v7, /device:TPU:103, one launch (start us, length us, event | category | flops | bytes accessed | tf_op | source)
XLA Modules:
  0.0 47.3 jit_solution(8988775859031582564)
XLA Ops:
  0.0 46.5 %shard_map.55 = f32[12,128,128]{2,1,0:T(8,128)S(1)} custom-call(f32[12,128,128]{2,1,0:T(8,128)} %bitcast.5, bf16[6,512,512]{2,1,0:T(8,128)(2,1)} %images.1, s32[3,2,6]{2,1,0:T(2,128)} %bitcast.6, s32[3,6]{1,0:T(4,128)} %bitcast.7, f32[6]{0:T(128)} %stiffness_hbm.1), custom_call_target="tpu_custom_call" | custom-call | tf_op jit(solution)/shard_map/pallas_call | solution.py:503
  46.5 0.9 %copy.7 = f32[6,2,128,128]{3,2,1,0:T(8,128)} copy(f32[6,2,128,128]{3,2,1,0:T(8,128)S(1)} %bitcast.4) | data formatting | bytes 1572864

commit v8 on v7

--- a/solution.py
+++ b/solution.py
@@ -427,9 +427,7 @@
 
         send_rims(0)
 
-    early = low_half & (me < lax.axis_size("sec") // 2)
-
-    @pl.when(jnp.logical_not(early))
+    @pl.when(high_half)
     def _():
         finishes(0, *edges)
         finishes(0, 2)
@@ -455,17 +453,22 @@
         passes(2, 4)
         finishes(2, 2, 3, 4, 0, 1)
 
-    @pl.when(early)
-    def _():
-        finishes(0, *inner)
-        for step in range(1, ITERS):
-            turns(step, *inner)
-            finishes(step - 1, *edges)
-            passes(step, *inner)
-            turns(step, *edges)
-            passes(step, *edges)
-            finishes(step, *inner)
-        finishes(ITERS - 1, *edges)
+    @pl.when(low_half)
+    def _():
+        finishes(0, *segments)
+        turns(1, *edges)
+        passes(1, *edges)
+        for seg in inner:
+            turns(1, seg)
+            passes(1, seg)
+        finishes(1, *inner)
+        turns(2, *inner)
+        finishes(1, *edges)
+        passes(2, *inner)
+        turns(2, *edges)
+        passes(2, *edges)
+        finishes(2, *inner)
+        finishes(2, *edges)
 
     for seg in segments:
         store(seg).wait()

time: 47.5 us -> 43.8 us (0.922)
  the two profiles are of different devices: /device:TPU:103 before, /device:TPU:56 now
where the time goes in v8:
time: 43.8 us; the launch traced here: 43.7 us
  Pallas kernels  42.8 us (98%)
  local copies, waits for them, and re-layouts  0.88 us (2%)
    pallas_call x1, Pallas kernels, local(): pl.pallas_call(kernel, out_shape=jax.ShapeDtypeStruct((FIELDS, GRID, GRID...  42.8 us
    unnamed x1, local copies, waits for them, and re-layouts  0.88 us

profile of v8, /device:TPU:56, one launch (start us, length us, event | category | flops | bytes accessed | tf_op | source)
XLA Modules:
  0.0 43.7 jit_solution(15578263509247141830)
XLA Ops:
  0.0 42.8 %shard_map.55 = f32[12,128,128]{2,1,0:T(8,128)S(1)} custom-call(f32[12,128,128]{2,1,0:T(8,128)} %bitcast.5, bf16[6,512,512]{2,1,0:T(8,128)(2,1)} %images.1, s32[3,2,6]{2,1,0:T(2,128)} %bitcast.6, s32[3,6]{1,0:T(4,128)} %bitcast.7, f32[6]{0:T(128)} %stiffness_hbm.1), custom_call_target="tpu_custom_call" | custom-call | tf_op jit(solution)/shard_map/pallas_call | solution.py:506
  42.8 0.9 %copy.7 = f32[6,2,128,128]{3,2,1,0:T(8,128)} copy(f32[6,2,128,128]{3,2,1,0:T(8,128)S(1)} %bitcast.4) | data formatting | bytes 1572864

commit v9 on v8

--- a/solution.py
+++ b/solution.py
@@ -462,8 +462,8 @@
             turns(1, seg)
             passes(1, seg)
         finishes(1, *inner)
+        finishes(1, *edges)
         turns(2, *inner)
-        finishes(1, *edges)
         passes(2, *inner)
         turns(2, *edges)
         passes(2, *edges)

time: 43.8 us -> 42.6 us (0.973)
  the two profiles are of different devices: /device:TPU:56 before, /device:TPU:30 now
where the time goes in v9:
time: 42.6 us; the launch traced here: 42.5 us
  Pallas kernels  41.6 us (98%)
  local copies, waits for them, and re-layouts  0.88 us (2%)
    pallas_call x1, Pallas kernels, local(): pl.pallas_call(kernel, out_shape=jax.ShapeDtypeStruct((FIELDS, GRID, GRID...  41.6 us
    unnamed x1, local copies, waits for them, and re-layouts  0.88 us

profile of v9, /device:TPU:30, one launch (start us, length us, event | category | flops | bytes accessed | tf_op | source)
XLA Modules:
  0.0 42.5 jit_solution(10611050758592772963)
XLA Ops:
  0.0 41.6 %shard_map.55 = f32[12,128,128]{2,1,0:T(8,128)S(1)} custom-call(f32[12,128,128]{2,1,0:T(8,128)} %bitcast.5, bf16[6,512,512]{2,1,0:T(8,128)(2,1)} %images.1, s32[3,2,6]{2,1,0:T(2,128)} %bitcast.6, s32[3,6]{1,0:T(4,128)} %bitcast.7, f32[6]{0:T(128)} %stiffness_hbm.1), custom_call_target="tpu_custom_call" | custom-call | tf_op jit(solution)/shard_map/pallas_call | solution.py:506
  41.6 0.9 %copy.7 = f32[6,2,128,128]{3,2,1,0:T(8,128)} copy(f32[6,2,128,128]{3,2,1,0:T(8,128)S(1)} %bitcast.4) | data formatting | bytes 1572864
